TPU v7x, 32 devices: a whole 2x2x4 slice. The times are simulated.
32 devices in a mesh: seq: 4 (over y, x), rep: 8 (over z, core).
Axes of the slice: x: 2, y: 2, z: 4, core: 2. Of those that a mesh axis runs over, the one named last changes fastest.
Arguments:
- long_input: bfloat16 [8, 2, 1024, 768], P('rep', None, 'seq'), may hold values from -6 to 6
- short_input: bfloat16 [8, 512, 768], P('rep', 'seq'), may hold values from -6 to 6
- long_cotangent: bfloat16 [8, 2, 1024, 768], P('rep', None, 'seq'), may hold values from -6 to 6
- short_cotangent: bfloat16 [8, 512, 768], P('rep', 'seq'), may hold values from -6 to 6
- doc_lengths: int32 [8, 4], P('rep'), may hold values from 1 to 256, 512 in all within a row
- master_attend: float32 [768, 2304], P('seq', 'rep'), may hold values from -0.21875 to 0.21875
- master_merge: float32 [768, 768], P('seq', 'rep'), may hold values from -0.875 to 0.875
- master_expand: float32 [768, 3072], P('seq', 'rep'), may hold values from -0.21875 to 0.21875
- master_contract: float32 [3072, 768], P('seq', 'rep'), may hold values from -0.109375 to 0.109375
- momentum_attend: float32 [768, 2304], P('seq', 'rep'), may hold values from -3.5 to 3.5
- momentum_merge: float32 [768, 768], P('seq', 'rep'), may hold values from -3.5 to 3.5
- momentum_expand: float32 [768, 3072], P('seq', 'rep'), may hold values from -8 to 8
- momentum_contract: float32 [3072, 768], P('seq', 'rep'), may hold values from -4 to 4
- error_attend: float32 [8, 768, 2304], P('rep', 'seq'), may hold values from -64 to 64
- error_merge: float32 [8, 768, 768], P('rep', 'seq'), may hold values from -64 to 64
- error_expand: float32 [8, 768, 3072], P('rep', 'seq'), may hold values from -160 to 160
- error_contract: float32 [8, 3072, 768], P('rep', 'seq'), may hold values from -160 to 160
- factor_attend: float32 [2304, 8], replicated, may hold values from -4 to 4
- factor_merge: float32 [768, 8], replicated, may hold values from -4 to 4
- factor_expand: float32 [3072, 8], replicated, may hold values from -4 to 4
- factor_contract: float32 [768, 8], replicated, may hold values from -4 to 4
- vector_params: float32 [9216], replicated, may hold values from -0.8 to 1.4, as said below
- vector_momentum: float32 [9216], replicated, may hold values from -56 to 56
Outputs:
- long_output: float32 [8, 2, 1024, 768], P('rep', None, 'seq')
- short_output: float32 [8, 512, 768], P('rep', 'seq')
- long_grad: float32 [8, 2, 1024, 768], P('rep', None, 'seq')
- short_grad: float32 [8, 512, 768], P('rep', 'seq')
- updated_attend: float32 [768, 2304], P('seq', 'rep')
- updated_merge: float32 [768, 768], P('seq', 'rep')
- updated_expand: float32 [768, 3072], P('seq', 'rep')
- updated_contract: float32 [3072, 768], P('seq', 'rep')
- momenta_attend: float32 [768, 2304], P('seq', 'rep')
- momenta_merge: float32 [768, 768], P('seq', 'rep')
- momenta_expand: float32 [768, 3072], P('seq', 'rep')
- momenta_contract: float32 [3072, 768], P('seq', 'rep')
- errors_attend: float32 [8, 768, 2304], P('rep', 'seq')
- errors_merge: float32 [8, 768, 768], P('rep', 'seq')
- errors_expand: float32 [8, 768, 3072], P('rep', 'seq')
- errors_contract: float32 [8, 3072, 768], P('rep', 'seq')
- factors_attend: float32 [2304, 8], replicated
- factors_merge: float32 [768, 8], replicated
- factors_expand: float32 [3072, 8], replicated
- factors_contract: float32 [768, 8], replicated
- updated_vectors: float32 [9216], replicated
- momenta_vectors: float32 [9216], replicated
Inputs may be any that keep to these rules, and one draw needn't show every extreme that they name: `doc_lengths`: each replica's 4 lengths sum to 512, and the largest of them is 256. `vector_params`: gain_one and gain_two lie in 0.6 to 1.4, the biases in -0.8 to 0.8.
All inputs are finite; a program needn't handle non-finite values.
Results may differ from a plain program's by a relative error of at most 0.014.
Values may be sent and summed in bfloat16 or wider, within the bound.
No kernel may reach another device: no remote copies, remote signals or barrier semaphores. Data moves between devices by JAX's collectives and lax.ppermute only.
A program may use at most 320 MiB of HBM per device.

v0:
```python
from functools import partial

import jax
import jax.numpy as jnp
from jax import lax
from jax.sharding import PartitionSpec as P

D = 768
HEADS = 12
HDIM = 64


LN_EPS = 1e-05
NORM_EPS = 1e-06
BETA = 0.9
RATE_MATRIX = 0.1
RATE_VECTOR = 0.01
MASKED = -1e30
HIGH = lax.Precision.HIGHEST


def layer_norm(values, gain, shift):
    center = values - jnp.mean(values, axis=-1, keepdims=True)
    spread = jnp.mean(center * center, axis=-1, keepdims=True)
    return center * lax.rsqrt(spread + LN_EPS) * gain + shift


def unpack(vectors):
    head = vectors[: 8 * D].reshape(8, D)
    return (
        head[0],
        head[1],
        head[2],
        head[3],
        head[4],
        head[5],
        head[6],
        head[7],
        vectors[8 * D :],
    )


def orthonormal(matrix):
    columns = []
    for column_id in range(matrix.shape[1]):
        column = matrix[:, column_id]
        for earlier in columns:
            column = column - jnp.sum(earlier * column) * earlier
        column = column * lax.rsqrt(jnp.sum(column * column) + NORM_EPS)
        columns.append(column)
    return jnp.stack(columns, axis=1)


def contract_rows(left, right, precision=None):
    return lax.dot_general(
        left,
        right,
        (((0,), (0,)), ((), ())),
        precision=precision,
        preferred_element_type=jnp.float32,
    )


def contract_cols(left, right, precision=None):
    return lax.dot_general(
        left,
        right,
        (((1,), (1,)), ((), ())),
        precision=precision,
        preferred_element_type=jnp.float32,
    )


def run_layer(tokens, cotangent, allowed, weights, vectors):
    w_attend, w_merge, w_expand, w_contract = weights
    (
        gain_one,
        shift_one,
        bias_query,
        bias_value,
        bias_merge,
        gain_two,
        shift_two,
        bias_contract,
        bias_expand,
    ) = unpack(vectors)
    batch, length = (tokens.shape[0], tokens.shape[1])
    rows_all = batch * length
    inputs = tokens.astype(jnp.float32).reshape(rows_all, D)
    normed_one, norm_one_back = jax.vjp(layer_norm, inputs, gain_one, shift_one)
    normed_low = normed_one.astype(jnp.bfloat16)
    joined = jnp.dot(normed_low, w_attend, preferred_element_type=jnp.float32)
    queries = (joined[:, :D] + bias_query).astype(jnp.bfloat16)
    keys_local = joined[:, D : 2 * D].astype(jnp.bfloat16)
    values_local = (joined[:, 2 * D :] + bias_value).astype(jnp.bfloat16)
    keys_all, values_all = (
        lax.all_gather(keys_local.reshape(batch, length, D), "seq", axis=1, tiled=True),
        lax.all_gather(values_local.reshape(batch, length, D), "seq", axis=1, tiled=True),
    )
    span = keys_all.shape[1]
    query_heads = queries.reshape(batch, length, HEADS, HDIM)
    key_heads = keys_all.reshape(batch, span, HEADS, HDIM)
    value_heads = values_all.reshape(batch, span, HEADS, HDIM)
    scale = HDIM ** (-0.5)

    def score_of():
        raw_scores = jnp.einsum(
            "bqhd,bkhd->bhqk", query_heads, key_heads, preferred_element_type=jnp.float32
        )
        return jnp.where(allowed, raw_scores * scale, MASKED)

    scores = score_of()
    row_top = jnp.max(scores, axis=-1, keepdims=True)
    expo = jnp.exp(scores - row_top)
    row_total = jnp.sum(expo, axis=-1, keepdims=True)
    soft_low = (expo / row_total).astype(jnp.bfloat16)
    log_total = row_top + jnp.log(row_total)
    mixed = (
        jnp.einsum("bhqk,bkhd->bqhd", soft_low, value_heads, preferred_element_type=jnp.float32)
        .astype(jnp.bfloat16)
        .reshape(rows_all, D)
    )
    middle = inputs + jnp.dot(mixed, w_merge, preferred_element_type=jnp.float32) + bias_merge
    normed_two, norm_two_back = jax.vjp(layer_norm, middle, gain_two, shift_two)
    hidden = normed_two.astype(jnp.bfloat16)
    expanded = jnp.dot(hidden, w_expand, preferred_element_type=jnp.float32) + bias_expand
    activated, gelu_back = jax.vjp(partial(jax.nn.gelu, approximate=True), expanded)
    active_low = activated.astype(jnp.bfloat16)
    output = (
        middle + jnp.dot(active_low, w_contract, preferred_element_type=jnp.float32) + bias_contract
    )
    grad_out = cotangent.astype(jnp.float32).reshape(rows_all, D)
    grad_out_low = cotangent.reshape(rows_all, D)
    contract_bias_grad = jnp.sum(grad_out, axis=0)
    grad_active = contract_cols(grad_out_low, w_contract)
    (grad_expanded,) = gelu_back(grad_active)
    expand_bias_grad = jnp.sum(grad_expanded, axis=0)
    expanded_low = grad_expanded.astype(jnp.bfloat16)
    grad_hidden = contract_cols(expanded_low, w_expand)
    middle_part, gain_two_grad, shift_two_grad = norm_two_back(grad_hidden)
    grad_middle = grad_out + middle_part
    merge_bias_grad = jnp.sum(grad_middle, axis=0)
    middle_low = grad_middle.astype(jnp.bfloat16)
    grad_mixed = (
        contract_cols(middle_low, w_merge).astype(jnp.bfloat16).reshape(batch, length, HEADS, HDIM)
    )
    soft_again = jnp.exp(score_of() - log_total)
    soft_again_low = soft_again.astype(jnp.bfloat16)
    values_grad_all = jnp.einsum(
        "bhqk,bqhd->bkhd", soft_again_low, grad_mixed, preferred_element_type=jnp.float32
    )
    grad_soft = jnp.einsum(
        "bqhd,bkhd->bhqk", grad_mixed, value_heads, preferred_element_type=jnp.float32
    )
    row_inner = jnp.sum(soft_again * grad_soft, axis=-1, keepdims=True)
    grad_scores = (soft_again * (grad_soft - row_inner) * scale).astype(jnp.bfloat16)
    grad_queries = jnp.einsum(
        "bhqk,bkhd->bqhd", grad_scores, key_heads, preferred_element_type=jnp.float32
    ).reshape(rows_all, D)
    keys_grad_all = jnp.einsum(
        "bhqk,bqhd->bkhd", grad_scores, query_heads, preferred_element_type=jnp.float32
    )
    keys_grad, values_grad = (
        lax.psum_scatter(
            keys_grad_all.reshape(batch, span, D), "seq", scatter_dimension=1, tiled=True
        ),
        lax.psum_scatter(
            values_grad_all.reshape(batch, span, D), "seq", scatter_dimension=1, tiled=True
        ),
    )
    keys_grad = keys_grad.reshape(rows_all, D)
    values_grad = values_grad.reshape(rows_all, D)
    query_bias_grad = jnp.sum(grad_queries, axis=0)
    value_bias_grad = jnp.sum(values_grad, axis=0)
    joined_low = jnp.concatenate([grad_queries, keys_grad, values_grad], axis=1).astype(
        jnp.bfloat16
    )
    grad_normed = contract_cols(joined_low, w_attend)
    input_part, gain_one_grad, shift_one_grad = norm_one_back(grad_normed)
    grad_input = grad_middle + input_part
    vector_grad = jnp.concatenate(
        [
            gain_one_grad,
            shift_one_grad,
            query_bias_grad,
            value_bias_grad,
            merge_bias_grad,
            gain_two_grad,
            shift_two_grad,
            contract_bias_grad,
            expand_bias_grad,
        ]
    )
    operands = (
        normed_low,
        joined_low,
        mixed,
        middle_low,
        hidden,
        expanded_low,
        active_low,
        grad_out_low,
    )
    return (
        output.reshape(batch, length, D),
        grad_input.reshape(batch, length, D),
        operands,
        vector_grad,
    )


def local(
    long_input,
    short_input,
    long_cotangent,
    short_cotangent,
    doc_lengths,
    master_attend,
    master_merge,
    master_expand,
    master_contract,
    momentum_attend,
    momentum_merge,
    momentum_expand,
    momentum_contract,
    error_attend,
    error_merge,
    error_expand,
    error_contract,
    factor_attend,
    factor_merge,
    factor_expand,
    factor_contract,
    vector_params,
    vector_momentum,
):
    masters = (master_attend, master_merge, master_expand, master_contract)
    widened = (
        lax.all_gather(master_attend.astype(jnp.bfloat16), "rep", axis=1, tiled=True),
        lax.all_gather(master_merge.astype(jnp.bfloat16), "rep", axis=1, tiled=True),
        lax.all_gather(master_expand.astype(jnp.bfloat16), "rep", axis=1, tiled=True),
        lax.all_gather(master_contract.astype(jnp.bfloat16), "rep", axis=1, tiled=True),
    )
    weights = (
        lax.all_gather(widened[0], "seq", axis=0, tiled=True),
        lax.all_gather(widened[1], "seq", axis=0, tiled=True),
        lax.all_gather(widened[2], "seq", axis=0, tiled=True),
        lax.all_gather(widened[3], "seq", axis=0, tiled=True),
    )
    seq_index = lax.axis_index("seq")
    seq_count = lax.axis_size("seq")
    rep_index = lax.axis_index("rep")
    rep_count = lax.axis_size("rep")
    long_tokens = long_input[0]
    long_length = long_tokens.shape[1]
    query_long = seq_index * long_length + jnp.arange(long_length, dtype=jnp.int32)
    key_long = jnp.arange(long_length * seq_count, dtype=jnp.int32)
    allowed_long = key_long[None, :] <= query_long[:, None]
    short_length = short_input.shape[1]
    query_short = seq_index * short_length + jnp.arange(short_length, dtype=jnp.int32)
    key_short = jnp.arange(short_length * seq_count, dtype=jnp.int32)
    doc_ends = jnp.cumsum(doc_lengths[0])
    query_doc = jnp.sum((query_short[:, None] >= doc_ends[None, :]).astype(jnp.int32), axis=1)
    key_doc = jnp.sum((key_short[:, None] >= doc_ends[None, :]).astype(jnp.int32), axis=1)
    allowed_short = (key_short[None, :] <= query_short[:, None]) & (
        key_doc[None, :] == query_doc[:, None]
    )
    long_result = run_layer(long_tokens, long_cotangent[0], allowed_long, weights, vector_params)
    short_result = run_layer(short_input, short_cotangent, allowed_short, weights, vector_params)
    operands = tuple(
        (
            jnp.concatenate([long_result[2][number], short_result[2][number]], axis=0)
            for number in range(8)
        )
    )
    local_grads = tuple(
        (contract_rows(operands[2 * number], operands[2 * number + 1]) for number in range(4))
    )
    summed = (
        lax.psum_scatter(
            local_grads[0].astype(jnp.bfloat16), "seq", scatter_dimension=0, tiled=True
        ).astype(jnp.float32),
        lax.psum_scatter(
            local_grads[1].astype(jnp.bfloat16), "seq", scatter_dimension=0, tiled=True
        ).astype(jnp.float32),
        lax.psum_scatter(
            local_grads[2].astype(jnp.bfloat16), "seq", scatter_dimension=0, tiled=True
        ).astype(jnp.float32),
        lax.psum_scatter(
            local_grads[3].astype(jnp.bfloat16), "seq", scatter_dimension=0, tiled=True
        ).astype(jnp.float32),
    )
    errors = (error_attend, error_merge, error_expand, error_contract)
    factors = (factor_attend, factor_merge, factor_expand, factor_contract)
    momenta = (momentum_attend, momentum_merge, momentum_expand, momentum_contract)
    corrected = [summed[number] + errors[number][0] for number in range(4)]
    projected = [
        jnp.dot(
            corrected[number], factors[number], precision=HIGH, preferred_element_type=jnp.float32
        )
        for number in range(4)
    ]
    reduced = lax.psum((projected[0], projected[1], projected[2], projected[3]), "rep")
    whole_p = (
        lax.all_gather(reduced[0].astype(jnp.bfloat16), "seq", axis=0, tiled=True).astype(
            jnp.float32
        ),
        lax.all_gather(reduced[1].astype(jnp.bfloat16), "seq", axis=0, tiled=True).astype(
            jnp.float32
        ),
        lax.all_gather(reduced[2].astype(jnp.bfloat16), "seq", axis=0, tiled=True).astype(
            jnp.float32
        ),
        lax.all_gather(reduced[3].astype(jnp.bfloat16), "seq", axis=0, tiled=True).astype(
            jnp.float32
        ),
    )
    basis_rows = []
    partial_q = []
    for number in range(4):
        basis = orthonormal(whole_p[number] / rep_count)
        height = corrected[number].shape[0]
        own_rows = lax.dynamic_slice_in_dim(basis, seq_index * height, height, 0)
        basis_rows.append(own_rows)
        partial_q.append(contract_rows(corrected[number], own_rows, HIGH))
    vector_total = long_result[3] + short_result[3]
    renewed_all = lax.psum(
        (partial_q[0], partial_q[1], partial_q[2], partial_q[3], vector_total), ("seq", "rep")
    )
    updated = []
    new_momenta = []
    new_errors = []
    new_factors = []
    for number in range(4):
        renewed = renewed_all[number] / rep_count
        approx = contract_cols(basis_rows[number], renewed, HIGH)
        new_errors.append((corrected[number] - approx)[None])
        width = masters[number].shape[1]
        own_block = lax.dynamic_slice_in_dim(approx, rep_index * width, width, 1)
        momentum_next = BETA * momenta[number] + own_block
        new_momenta.append(momentum_next)
        updated.append(masters[number] - RATE_MATRIX * momentum_next)
        new_factors.append(renewed)
    vector_grad = renewed_all[4] / rep_count
    momenta_vectors = BETA * vector_momentum + vector_grad
    updated_vectors = vector_params - RATE_VECTOR * momenta_vectors
    long_output = long_result[0].reshape(long_input.shape)
    long_grad = long_result[1].reshape(long_input.shape)
    return (
        long_output,
        short_result[0],
        long_grad,
        short_result[1],
        updated[0],
        updated[1],
        updated[2],
        updated[3],
        new_momenta[0],
        new_momenta[1],
        new_momenta[2],
        new_momenta[3],
        new_errors[0],
        new_errors[1],
        new_errors[2],
        new_errors[3],
        new_factors[0],
        new_factors[1],
        new_factors[2],
        new_factors[3],
        updated_vectors,
        momenta_vectors,
    )


def solution(mesh):
    in_specs = (
        P("rep", None, "seq", None),
        P("rep", "seq", None),
        P("rep", None, "seq", None),
        P("rep", "seq", None),
        P("rep", None),
        P("seq", "rep"),
        P("seq", "rep"),
        P("seq", "rep"),
        P("seq", "rep"),
        P("seq", "rep"),
        P("seq", "rep"),
        P("seq", "rep"),
        P("seq", "rep"),
        P("rep", "seq", None),
        P("rep", "seq", None),
        P("rep", "seq", None),
        P("rep", "seq", None),
        P(),
        P(),
        P(),
        P(),
        P(),
        P(),
    )
    out_specs = (
        P("rep", None, "seq", None),
        P("rep", "seq", None),
        P("rep", None, "seq", None),
        P("rep", "seq", None),
        P("seq", "rep"),
        P("seq", "rep"),
        P("seq", "rep"),
        P("seq", "rep"),
        P("seq", "rep"),
        P("seq", "rep"),
        P("seq", "rep"),
        P("seq", "rep"),
        P("rep", "seq", None),
        P("rep", "seq", None),
        P("rep", "seq", None),
        P("rep", "seq", None),
        P(),
        P(),
        P(),
        P(),
        P(),
        P(),
    )
    return jax.shard_map(local, mesh=mesh, in_specs=in_specs, out_specs=out_specs, check_vma=False)
```

profile of v0, /device:TPU:0, one launch (start us, length us, event | category | flops | bytes accessed | tf_op | source)
XLA Modules:
  0.0 1367.3 jit_solution(15832527662573305666)
XLA Ops:
  11.8 24.7 %all_gather.48 = bf16[192,2304]{0,1:T(8,128)(2,1)S(1)} all-gather(bf16[192,288]{0,1:T(8,128)(2,1)S(1)} %copy.134), channel_id=1, replica_groups=mesh['seq'=4,'rep'=8] {'rep'}, dimensions={1}, use_global_device_ids=true | all-gather | bytes 995328 | tf_op jit(solution)/shard_map/all_gather | solution.py:239
  38.0 14.4 %all_gather.52 = bf16[192,768]{0,1:T(8,128)(2,1)S(1)} all-gather(bf16[192,96]{0,1:T(8,128)(2,1)S(1)} %copy.141), channel_id=1, replica_groups=mesh['seq'=4,'rep'=8] {'rep'}, dimensions={1}, use_global_device_ids=true | all-gather | bytes 331776 | tf_op jit(solution)/shard_map/all_gather | solution.py:240
  54.0 10.9 all-gather.26.cloned.1.call-done
  67.2 47.0 %all-gather.14.cloned.1.call-done = bf16[768,2304]{1,0:T(8,128)(2,1)} async-done(((bf16[192,2304]{1,0:T(8,128)(2,1)}), bf16[768,2304]{1,0:T(8,128)(2,1)}) %all-gather.14.cloned.1.call-update) | async-done | bytes 3538960 | tf_op jit(solution)/shard_map/all_gather | solution.py:245
  126.8 11.9 all-gather.1
  139.9 11.4 all-gather
  165.3 39.1 %all-gather.24.cloned.1.call-done = bf16[768,3072]{1,0:T(8,128)(2,1)} async-done(((bf16[192,3072]{1,0:T(8,128)(2,1)}), bf16[768,3072]{1,0:T(8,128)(2,1)}) %all-gather.24.cloned.1.call-update) | async-done | bytes 4718608 | tf_op jit(solution)/shard_map/all_gather | solution.py:247
  209.5 53.6 %all-gather.28.cloned.1.call-done = bf16[3072,768]{0,1:T(8,128)(2,1)} async-done(((bf16[768,768]{0,1:T(8,128)(2,1)}), bf16[3072,768]{0,1:T(8,128)(2,1)}) %all-gather.28.cloned.1.call-update) | async-done | bytes 4718608 | tf_op jit(solution)/shard_map/all_gather | solution.py:248
  286.5 12.9 fusion.45
  299.7 9.1 all-gather.18.cloned.1.call-done
  313.5 14.7 %fusion.4 = (f32[2,12,256]{2,1,0:T(8,128)S(1)}, f32[2,12,256,1024]{3,2,1,0:T(8,128)}) fusion(pred[256,1024]{1,0:T(8,128)(4,1)S(1)} %iota_compare_fusion, bf16[2,1024,12,64]{1,3,2,0:T(8,128)(2,1)} %bitcast.269, bf16[2,256,12,64]{1,0,3,2:T(2,128)(2,1)} %reshape.438), kind=kOutput, calls=%fused_computation.10 | convolution fusion | flops 824174592 | bytes 29384704 | tf_op jit(solution)/shard_map/bqhd,bkhd->bhqk/dot_general | solution.py:107
  328.2 12.4 fusion.3
  340.7 14.5 %all-gather.16.cloned.1.call-done = bf16[2,1024,768]{2,1,0:T(8,128)(2,1)} async-done(((bf16[2,256,768]{2,1,0:T(8,128)(2,1)}), bf16[2,1024,768]{2,1,0:T(8,128)(2,1)}) %all-gather.16.cloned.1.call-update) | async-done | bytes 3145744 | tf_op jit(solution)/shard_map/all_gather | solution.py:98
  359.8 13.1 fusion.87
  379.9 8.6 fusion.206
  403.4 13.9 %fusion.5 = f32[2,12,64,1024]{3,2,1,0:T(8,128)} fusion(f32[2,12,256,1024]{3,2,1,0:T(8,128)} %get-tuple-element.343, f32[2,12,256]{2,1,0:T(8,128)S(1)} %log_add_fusion, pred[256,1024]{1,0:T(8,128)(4,1)S(1)} %iota_compare_fusion, bf16[2,256,12,64]{1,0,3,2:T(2,128)(2,1)} %reshape.452), kind=kOutput, calls=%fused_computation.11 | convolution fusion | flops 830472192 | bytes 32530432 | tf_op jit(solution)/shard_map/bhqk,bqhd->bkhd/dot_general | solution.py:149
  423.9 15.0 %fusion.115 = f32[2,12,256,1024]{3,2,1,0:T(8,128)} fusion(bf16[2,1024,12,64]{1,3,2,0:T(8,128)(2,1)} %bitcast.266, bf16[2,256,12,64]{1,0,3,2:T(2,128)(2,1)} %reshape.452), kind=kOutput, calls=%fused_computation.151 | convolution fusion | flops 805306368 | bytes 29097984 | tf_op jit(solution)/shard_map/bqhd,bkhd->bhqk/dot_general | solution.py:152
  438.9 47.1 %fusion.11 = f32[2,12,64,1024]{3,2,1,0:T(8,128)} fusion(f32[2,12,256,1024]{3,2,1,0:T(8,128)} %fusion.115, f32[2,12,256,1024]{3,2,1,0:T(8,128)} %get-tuple-element.343, f32[2,12,256]{2,1,0:T(8,128)S(1)} %copy-done.86, pred[256,1024]{1,0:T(8,128)(4,1)S(1)} %iota_compare_fusion, bf16[2,256,12,64]{1,0,3,2:T(2,128)(2,1)} %reshape.438), kind=kOutput, calls=%fused_computation.14 | convolution fusion | flops 874519552 | bytes 57696256 | tf_op jit(solution)/shard_map/bhqk,bqhd->bkhd/dot_general | solution.py:160
  496.6 8.5 convolution_convert_fusion
  505.2 9.1 convolution_convert_fusion.1
  517.9 13.6 fusion.216
  532.2 52.3 %bitcast_convert_fusion = (bf16[2,256,12,64]{1,3,2,0:T(8,128)(2,1)S(1)}, f32[2,12,64,256]{3,2,1,0:T(8,128)}) fusion(bf16[2,1024,12,64]{1,3,2,0:T(8,128)(2,1)} %bitcast.270, f32[2,12,256,1024]{3,2,1,0:T(8,128)} %fusion.115, f32[2,12,256]{2,1,0:T(8,128)} %copy-done.85, f32[2,12,256,1024]{3,2,1,0:T(8,128)} %get-tuple-element.343, ...), kind=kOutput, calls=%fused_computation.86 | convolution fusion | flops 874912768 | bytes 56123392 | tf_op jit(solution)/shard_map/bhqk,bkhd->bqhd/dot_general | solution.py:157
  619.6 42.6 %reduce-scatter.23.cloned.1.call-done = bf16[768,768]{1,0:T(8,128)(2,1)} async-done(((bf16[3072,768]{1,0:T(8,128)(2,1)}), bf16[768,768]{1,0:T(8,128)(2,1)}) %reduce-scatter.23.cloned.1.call-update) | async-done | bytes 1179664 | tf_op jit(solution)/shard_map/reduce_scatter | solution.py:289
  665.6 56.4 %reduce-scatter.21.cloned.1.call-done = bf16[192,3072]{1,0:T(8,128)(2,1)} async-done(((bf16[768,3072]{1,0:T(8,128)(2,1)}), bf16[192,3072]{1,0:T(8,128)(2,1)}) %reduce-scatter.21.cloned.1.call-update) | async-done | bytes 1179664 | tf_op jit(solution)/shard_map/reduce_scatter | solution.py:286
  734.1 38.0 %reduce-scatter.17.cloned.1.call-done = bf16[192,2304]{1,0:T(8,128)(2,1)} async-done(((bf16[768,2304]{1,0:T(8,128)(2,1)}), bf16[192,2304]{1,0:T(8,128)(2,1)}) %reduce-scatter.17.cloned.1.call-update) | async-done | bytes 884752 | tf_op jit(solution)/shard_map/reduce_scatter | solution.py:280
  775.4 28.9 %all-reduce.2 = (bf16[192,8]{0,1:T(8,128)(2,1)S(1)}, bf16[192,8]{0,1:T(8,128)(2,1)S(1)}, bf16[192,8]{0,1:T(8,128)(2,1)S(1)}, bf16[768,8]{0,1:T(8,128)(2,1)S(1)}) all-reduce(f32[192,8]{0,1:T(8,128)S(1)} %fusion.121, f32[192,8]{0,1:T(8,128)S(1)} %fusion.111, f32[192,8]{0,1:T(8,128)S(1)} %fusion.145, ...), channel_id=1, replica_groups=mesh['seq'=4,'rep'=8] {'rep'}, use_global_device_ids=true, to_apply=%region_30.31 | all-reduce | flops 10752 | bytes 64512 | tf_op jit(solution)/shard_map/psum | solution.py:303
  1014.1 18.0 %subtract_multiply_fusion = (f32[3072,1]{0,1:T(1,128)S(1)}, f32[3072,1]{0,1:T(1,128)S(1)}, f32[3072,1]{0,1:T(1,128)}, f32[3072,1]{0,1:T(1,128)}, f32[3072,1]{0,1...) fusion(f32[3072,1]{0,1:T(1,128)S(1)} %get-tuple-element.325, f32[]{:T(128)S(6)} %rsqrt.171, f32[]{:T(128)} %get-tuple-element.194, ...), kind=kLoop, calls=%fused_computation.222 | loop fusion | flops 193536 | bytes 184460 | tf_op jit(solution)/shard_map/mul | solution.py:49
  1032.1 18.3 %subtract_multiply_fusion.14 = (f32[768,1]{0,1:T(1,128)S(1)}, f32[768,1]{0,1:T(1,128)S(1)}, f32[768,1]{0,1:T(1,128)S(1)}, f32[768,1]{0,1:T(1,128)S(1)}, f32[768,...) fusion(f32[768,1]{0,1:T(1,128)} %get-tuple-element.242, f32[768,8]{0,1:T(8,128)} %copy-done.58, ...), kind=kLoop, calls=%fused_computation.523 | loop fusion | flops 48384 | bytes 46220 | tf_op jit(solution)/shard_map/mul | solution.py:49
  1050.4 19.0 %subtract_multiply_fusion.7 = (f32[768,1]{0,1:T(1,128)}, f32[768,1]{0,1:T(1,128)}, f32[768,1]{0,1:T(1,128)}, f32[768,1]{0,1:T(1,128)}, f32[768,1]{0,1:T(1,128)}, /*index=5*/f32[768,1]{0,1:T(1,128)}, f32[768,1]{0,1:T(1,128)}) fusion(f32[768,1]{0,1:T(1,128)} %get-tuple-element.361, f32[768,8]{0,1:T(8,128)S(1)} %reshape.486, f32[]{:T(128)S(6)} %rsqrt.163, ...), kind=kLoop, calls=%fused_computation.515 | loop fusion | flops 48384 | bytes 46220 | tf_op jit(solution)/shard_map/mul | solution.py:49
  1069.4 18.3 %subtract_multiply_fusion.21 = (f32[768,1]{0,1:T(1,128)}, f32[768,1]{0,1:T(1,128)}, f32[768,1]{0,1:T(1,128)}, f32[768,1]{0,1:T(1,128)}, f32[768,1]{0,1:T(1,128)}, /*index=5*/f32[768,1]{0,1:T(1,128)}, f32[768,1]{0,1:T(1,128)}) fusion(f32[768,1]{0,1:T(1,128)S(1)} %get-tuple-element.302, f32[768,8]{0,1:T(8,128)S(1)} %reshape.482, f32[]{:T(128)S(6)} %rsqrt.147, ...), kind=kLoop, calls=%fused_computation.531 | loop fusion | flops 48384 | bytes 46220 | tf_op jit(solution)/shard_map/mul | solution.py:49
  1100.6 113.9 %all-reduce.6.cloned.1.call-done = (f32[768,8]{0,1:T(8,128)}, f32[768,8]{0,1:T(8,128)}, f32[9216]{0:T(1024)}) async-done(((f32[768,8]{0,1:T(8,128)}, f32[768,8]{0,1:T(8,128)}, f32[9216]{0:T(1024)}), (f32[768,8]{0,1:T(8,128)}, f32[768,8]{0,1:T(8,128)}, f32[9216]{0:T(1024)})) %all-reduce.6.cloned.1.call-update) | async-done | bytes 86032 | tf_op jit(solution)/shard_map/psum | solution.py:327
  1233.7 112.7 %all-reduce.8.cloned.1.call-done = (f32[2304,8]{0,1:T(8,128)}, f32[3072,8]{0,1:T(8,128)}) async-done(((f32[2304,8]{0,1:T(8,128)}, f32[3072,8]{0,1:T(8,128)}), (f32[2304,8]{0,1:T(8,128)}, f32[3072,8]{0,1:T(8,128)})) %all-reduce.8.cloned.1.call-update) | async-done | bytes 172048 | tf_op jit(solution)/shard_map/psum | solution.py:327
  (551 shorter events, 404.5 us)
Async XLA Ops:
  7.2 714.8 %copy-start = (f32[3072,8]{0,1:T(8,128)S(1)}, f32[3072,8]{0,1:T(8,128)}, u32[]{:S(2)}) copy-start(f32[3072,8]{0,1:T(8,128)} %param.42) | copy-start | bytes 294916
  7.2 46.2 %all-gather.22.cloned.1.call-start = ((), (), s32[]{:S(2)}) async-start(), calls=%async_computation.12 | async-start | bytes 1327104 | tf_op jit(solution)/shard_map/all_gather | solution.py:241
  9.0 55.9 %all-gather.26.cloned.1.call-start = ((), (), s32[]{:S(2)}) async-start(), calls=%async_computation.14 | async-start | bytes 1327104 | tf_op jit(solution)/shard_map/all_gather | solution.py:242
  10.7 103.4 %all-gather.14.cloned.1.call-start = ((), (), s32[]{:S(2)}) async-start(), calls=%async_computation.8 | async-start | bytes 4423680 | tf_op jit(solution)/shard_map/all_gather | solution.py:245
  37.8 124.0 %all-gather.20.cloned.1.call-start = ((), (), s32[]{:S(2)}) async-start(), calls=%async_computation.11 | async-start | bytes 1474560 | tf_op jit(solution)/shard_map/all_gather | solution.py:246
  53.3 151.1 %all-gather.24.cloned.1.call-start = ((), (), s32[]{:S(2)}) async-start(), calls=%async_computation.13 | async-start | bytes 5898240 | tf_op jit(solution)/shard_map/all_gather | solution.py:247
  53.9 209.2 %all-gather.28.cloned.1.call-start = ((), (), s32[]{:S(2)}) async-start(), calls=%async_computation.15 | async-start | bytes 5898240 | tf_op jit(solution)/shard_map/all_gather | solution.py:248
  64.9 243.9 %all-gather.18.cloned.1.call-start = ((), (), s32[]{:S(2)}) async-start(), calls=%async_computation.10 | async-start | bytes 3932160 | tf_op jit(solution)/shard_map/all_gather | solution.py:97
  66.8 56.0 %copy-start.59 = (f32[768]{0:T(1024)}, f32[768]{0:T(1024)S(1)}, u32[]{:S(2)}) copy-start(f32[768]{0:T(1024)S(1)} %get-tuple-element.339) | copy-start | bytes 9220
  66.8 95.1 %copy-start.92 = (f32[768]{0:T(1024)}, f32[768]{0:T(1024)S(1)}, u32[]{:S(2)}) copy-start(f32[768]{0:T(1024)S(1)} %get-tuple-element.335) | copy-start | bytes 9220
  67.2 55.1 %copy-start.22 = (bf16[1,128,768]{2,1,0:T(8,128)(2,1)S(1)}, bf16[1,128,768]{2,1,0:T(8,128)(2,1)}, u32[]{:S(2)}) copy-start(bf16[1,128,768]{2,1,0:T(8,128)(2,1)} %param.24) | copy-start | bytes 589828
  121.3 233.9 %all-gather.16.cloned.1.call-start = ((), (), s32[]{:S(2)}) async-start(), calls=%async_computation.9 | async-start | bytes 3932160 | tf_op jit(solution)/shard_map/all_gather | solution.py:98
  158.9 426.7 %reduce-scatter.15.cloned.1.call-start = ((), (), s32[]{:S(2)}) async-start(), calls=%async_computation.19 | async-start | bytes 1966080 | tf_op jit(solution)/shard_map/reduce_scatter | solution.py:167
  165.3 97.8 %copy-start.36 = (bf16[1,128,768]{2,1,0:T(8,128)(2,1)S(1)}, bf16[1,128,768]{2,1,0:T(8,128)(2,1)}, u32[]{:S(2)}) copy-start(bf16[1,128,768]{2,1,0:T(8,128)(2,1)} %param.26) | copy-start | bytes 589828
  277.5 310.2 %reduce-scatter.13.cloned.1.call-start = ((), (), s32[]{:S(2)}) async-start(), calls=%async_computation.18 | async-start | bytes 1966080 | tf_op jit(solution)/shard_map/reduce_scatter | solution.py:164
  299.4 290.0 %reduce-scatter.11.cloned.1.call-start = ((), (), s32[]{:S(2)}) async-start(), calls=%async_computation.17 | async-start | bytes 7864320 | tf_op jit(solution)/shard_map/reduce_scatter | solution.py:167
  423.9 168.0 %reduce-scatter.9.cloned.1.call-start = ((), (), s32[]{:S(2)}) async-start(), calls=%async_computation.16 | async-start | bytes 7864320 | tf_op jit(solution)/shard_map/reduce_scatter | solution.py:164
  492.5 125.5 %reduce-scatter.19.cloned.1.call-start = ((), (), s32[]{:S(2)}) async-start(), calls=%async_computation.21 | async-start | bytes 1474560 | tf_op jit(solution)/shard_map/reduce_scatter | solution.py:283
  496.5 165.7 %reduce-scatter.23.cloned.1.call-start = ((), (), s32[]{:S(2)}) async-start(), calls=%async_computation.23 | async-start | bytes 5898240 | tf_op jit(solution)/shard_map/reduce_scatter | solution.py:289
  505.1 216.9 %reduce-scatter.21.cloned.1.call-start = ((), (), s32[]{:S(2)}) async-start(), calls=%async_computation.22 | async-start | bytes 5898240 | tf_op jit(solution)/shard_map/reduce_scatter | solution.py:286
  514.3 257.8 %reduce-scatter.17.cloned.1.call-start = ((), (), s32[]{:S(2)}) async-start(), calls=%async_computation.20 | async-start | bytes 4423680 | tf_op jit(solution)/shard_map/reduce_scatter | solution.py:280
  601.2 613.4 %all-reduce.6.cloned.1.call-start = ((), (), s32[]{:S(2)}) async-start(), calls=%async_computation.24 | async-start | bytes 172032 | tf_op jit(solution)/shard_map/psum | solution.py:327
  619.6 106.5 %copy-start.5 = (bf16[1,2,256,768]{3,2,1,0:T(8,128)(2,1)S(1)}, bf16[1,2,256,768]{3,2,1,0:T(8,128)(2,1)}, u32[]{:S(2)}) copy-start(bf16[1,2,256,768]{3,2,1,0:T(8,128)(2,1)} %param.23) | copy-start | bytes 2359300
  619.6 106.6 %copy-start.82 = (f32[1,2,2,128]{3,1,2,0:T(2,128)S(1)}, f32[1,2,2,128]{3,1,2,0:T(2,128)}, u32[]{:S(2)}) copy-start(f32[1,2,2,128]{3,1,2,0:T(2,128)} %copy-done.81) | copy-start | bytes 6148
  734.1 355.3 %copy-start.25 = (f32[1,192,768]{2,1,0:T(8,128)S(1)}, f32[1,192,768]{2,1,0:T(8,128)}, u32[]{:S(2)}) copy-start(f32[1,192,768]{2,1,0:T(8,128)} %param.37) | copy-start | bytes 1769476
  734.1 355.3 %copy-start.34 = (bf16[192,768]{1,0:T(8,128)(2,1)S(1)}, bf16[192,768]{1,0:T(8,128)(2,1)}, u32[]{:S(2)}) copy-start(bf16[192,768]{1,0:T(8,128)(2,1)} %reduce-scatter.19.cloned.1.call-done) | copy-start | bytes 884740
  828.0 128.1 %copy-start.58 = (f32[768,8]{0,1:T(8,128)}, f32[768,8]{0,1:T(8,128)S(1)}, u32[]{:S(2)}) copy-start(f32[768,8]{0,1:T(8,128)S(1)} %reshape.484) | copy-start | bytes 73732
  1094.0 252.4 %all-reduce.8.cloned.1.call-start = ((), (), s32[]{:S(2)}) async-start(), calls=%async_computation.25 | async-start | bytes 344064 | tf_op jit(solution)/shard_map/psum | solution.py:327
  1231.9 121.7 %copy-start.39 = (f32[192,288]{1,0:T(8,128)S(1)}, f32[192,288]{1,0:T(8,128)}, u32[]{:S(2)}) copy-start(f32[192,288]{1,0:T(8,128)} %param.28) | copy-start | bytes 663556
  1231.9 121.7 %copy-start.56 = (f32[192,288]{1,0:T(8,128)S(1)}, f32[192,288]{1,0:T(8,128)}, u32[]{:S(2)}) copy-start(f32[192,288]{1,0:T(8,128)} %param.32) | copy-start | bytes 663556
  1233.7 120.9 %copy-start.40 = (f32[192,384]{1,0:T(8,128)S(1)}, f32[192,384]{1,0:T(8,128)}, u32[]{:S(2)}) copy-start(f32[192,384]{1,0:T(8,128)} %param.30) | copy-start | bytes 884740
  1233.7 120.9 %copy-start.57 = (f32[192,384]{1,0:T(8,128)S(1)}, f32[192,384]{1,0:T(8,128)}, u32[]{:S(2)}) copy-start(f32[192,384]{1,0:T(8,128)} %param.34) | copy-start | bytes 884740
  (122 other events, 1090.7 us)
Sparse Core Ops, SparseCore 0:
  10.2 30.1 all-gather.21
  42.6 22.2 all-gather.25
  67.3 46.7 all-gather.13
  116.4 29.3 all-gather.19
  147.4 56.9 all-gather.23
  206.1 56.9 all-gather.27
  264.9 43.8 all-gather.17
  311.3 43.8 all-gather.15
  358.7 31.1 reduce-scatter.14
  393.3 31.1 reduce-scatter.12
  427.5 70.0 reduce-scatter.10
  500.5 70.0 reduce-scatter.8
  573.5 28.7 reduce-scatter.18
  605.2 56.9 reduce-scatter.22
  665.0 56.9 reduce-scatter.20
  725.0 47.1 reduce-scatter.16
  1094.2 120.3 all-reduce.5
  1220.6 125.7 all-reduce.7
where the time goes:
time: 1380 us; the launch traced here: 1370 us
  waiting for transfers between devices  539 us (39%)
  matrix products  312 us (23%)
  other arithmetic  290 us (21%)
  blocking collectives  122 us (9%)
  local copies, waits for them, and re-layouts  63.9 us (5%)
  between operations  38.8 us (3%)
    psum x2, waiting for transfers between devices, local(): lax.psum((partial_q[0], partial_q[1], partial_q[2], partial_q[3], vector_...  227 us
    reduce_sum x36, other arithmetic, orthonormal(): column = column - jnp.sum(earlier * column) * earlier  117 us
    mul x6, other arithmetic, orthonormal(): column = column * lax.rsqrt(jnp.sum(column * column) + NORM_EPS)  74.2 us
    dot_general x2, matrix products, run_layer(): jnp.einsum('bhqk,bkhd->bqhd', grad_scores, key_heads, preferred_element_t...  65.9 us
    dot_general x2, matrix products, run_layer(): jnp.einsum('bhqk,bqhd->bkhd', grad_scores, query_heads, preferred_element...  60 us
    reduce_scatter x1, waiting for transfers between devices, local(): lax.psum_scatter(local_grads[2].astype(jnp.bfloat16), 'seq', scatter_dime...  56.4 us
    all_gather x1, waiting for transfers between devices, local(): lax.all_gather(widened[3], 'seq', axis=0, tiled=True)  53.6 us
    all_gather x1, waiting for transfers between devices, local(): lax.all_gather(widened[0], 'seq', axis=0, tiled=True)  47 us
  transfers between devices with their start and end apart: 18, of which 11 were waited for; matrix products, arithmetic and copies ran while one was open for 29% of the time, Pallas kernels for 0%

commit v1 on v0

--- a/solution.py
+++ b/solution.py
@@ -3,11 +3,13 @@
 import jax
 import jax.numpy as jnp
 from jax import lax
+from jax.experimental import pallas as pl
 from jax.sharding import PartitionSpec as P
 
 D = 768
 HEADS = 12
 HDIM = 64
+LANES = 128
 
 
 LN_EPS = 1e-05
@@ -40,15 +42,31 @@
     )
 
 
-def orthonormal(matrix):
-    columns = []
-    for column_id in range(matrix.shape[1]):
-        column = matrix[:, column_id]
-        for earlier in columns:
-            column = column - jnp.sum(earlier * column) * earlier
-        column = column * lax.rsqrt(jnp.sum(column * column) + NORM_EPS)
-        columns.append(column)
-    return jnp.stack(columns, axis=1)
+def orthonormal(gathered, widths, scale):
+    rank = gathered.shape[1]
+
+    def kernel(p_ref, basis_ref):
+        offset = 0
+        for width in widths:
+            block = p_ref[:, :, offset : offset + width] * scale
+            row_ids = lax.broadcasted_iota(jnp.int32, (1, rank, 1), 1)
+            for column_id in range(rank):
+                column = block[:, column_id : column_id + 1, :]
+                length = jnp.sum(
+                    jnp.sum(column * column, axis=2, keepdims=True), axis=0, keepdims=True
+                )
+                unit = column * lax.rsqrt(length + NORM_EPS)
+                inner = jnp.sum(
+                    jnp.sum(block * unit, axis=2, keepdims=True), axis=0, keepdims=True
+                )
+                later = jnp.where(row_ids > column_id, inner, 0.0)
+                block = jnp.where(row_ids == column_id, unit, block - later * unit)
+            basis_ref[:, :, offset : offset + width] = block
+            offset += width
+
+    return pl.pallas_call(
+        kernel, out_shape=jax.ShapeDtypeStruct(gathered.shape, jnp.float32), name="orthonormal"
+    )(gathered)
 
 
 def contract_rows(left, right, precision=None):
@@ -294,54 +312,64 @@
     factors = (factor_attend, factor_merge, factor_expand, factor_contract)
     momenta = (momentum_attend, momentum_merge, momentum_expand, momentum_contract)
     corrected = [summed[number] + errors[number][0] for number in range(4)]
-    projected = [
-        jnp.dot(
-            corrected[number], factors[number], precision=HIGH, preferred_element_type=jnp.float32
-        )
-        for number in range(4)
-    ]
-    reduced = lax.psum((projected[0], projected[1], projected[2], projected[3]), "rep")
-    whole_p = (
-        lax.all_gather(reduced[0].astype(jnp.bfloat16), "seq", axis=0, tiled=True).astype(
-            jnp.float32
-        ),
-        lax.all_gather(reduced[1].astype(jnp.bfloat16), "seq", axis=0, tiled=True).astype(
-            jnp.float32
-        ),
-        lax.all_gather(reduced[2].astype(jnp.bfloat16), "seq", axis=0, tiled=True).astype(
-            jnp.float32
-        ),
-        lax.all_gather(reduced[3].astype(jnp.bfloat16), "seq", axis=0, tiled=True).astype(
-            jnp.float32
-        ),
-    )
+    heights = [corrected[number].shape[0] for number in range(4)]
+    padded = [-(-height // LANES) * LANES for height in heights]
+    projected = jnp.concatenate(
+        [
+            jnp.pad(
+                lax.dot_general(
+                    factors[number],
+                    corrected[number],
+                    (((0,), (1,)), ((), ())),
+                    precision=HIGH,
+                    preferred_element_type=jnp.float32,
+                ),
+                ((0, 0), (0, padded[number] - heights[number])),
+            )
+            for number in range(4)
+        ],
+        axis=1,
+    )
+    reduced = lax.psum(projected, "rep")
+    whole_p = lax.all_gather(reduced, "seq", axis=0, tiled=False)
+    basis_all = orthonormal(whole_p, padded, 1.0 / rep_count)
+    basis_own = lax.dynamic_index_in_dim(basis_all, seq_index, 0, keepdims=False)
     basis_rows = []
     partial_q = []
+    offset = 0
     for number in range(4):
-        basis = orthonormal(whole_p[number] / rep_count)
-        height = corrected[number].shape[0]
-        own_rows = lax.dynamic_slice_in_dim(basis, seq_index * height, height, 0)
+        own_rows = basis_own[:, offset : offset + heights[number]]
+        offset += padded[number]
         basis_rows.append(own_rows)
-        partial_q.append(contract_rows(corrected[number], own_rows, HIGH))
+        partial_q.append(
+            jnp.dot(
+                own_rows, corrected[number], precision=HIGH, preferred_element_type=jnp.float32
+            )
+        )
+    rank = projected.shape[0]
     vector_total = long_result[3] + short_result[3]
     renewed_all = lax.psum(
-        (partial_q[0], partial_q[1], partial_q[2], partial_q[3], vector_total), ("seq", "rep")
-    )
+        jnp.concatenate(partial_q + [vector_total.reshape(rank, -1)], axis=1), ("seq", "rep")
+    )
+    renewed_all = renewed_all / rep_count
     updated = []
     new_momenta = []
     new_errors = []
     new_factors = []
+    offset = 0
     for number in range(4):
-        renewed = renewed_all[number] / rep_count
-        approx = contract_cols(basis_rows[number], renewed, HIGH)
+        columns = corrected[number].shape[1]
+        renewed = renewed_all[:, offset : offset + columns]
+        offset += columns
+        approx = contract_rows(basis_rows[number], renewed, HIGH)
         new_errors.append((corrected[number] - approx)[None])
         width = masters[number].shape[1]
         own_block = lax.dynamic_slice_in_dim(approx, rep_index * width, width, 1)
         momentum_next = BETA * momenta[number] + own_block
         new_momenta.append(momentum_next)
         updated.append(masters[number] - RATE_MATRIX * momentum_next)
-        new_factors.append(renewed)
-    vector_grad = renewed_all[4] / rep_count
+        new_factors.append(renewed.T)
+    vector_grad = renewed_all[:, offset:].reshape(vector_total.shape)
     momenta_vectors = BETA * vector_momentum + vector_grad
     updated_vectors = vector_params - RATE_VECTOR * momenta_vectors
     long_output = long_result[0].reshape(long_input.shape)

time: 1380 us -> 1010 us (0.73)
  other arithmetic: 290 us -> 62.4 us
  waiting for transfers between devices: 539 us -> 433 us
  between operations: 38.8 us -> 15.6 us
  blocking collectives: 122 us -> 102 us
    reduce_sum x57 -> x0, other arithmetic: 153 us -> none  [the longest x36 117 us: orthonormal(): column = column - jnp.sum(earlier * column) * earlier]
    psum x2 -> x1, waiting for transfers between devices: 227 us -> 120 us  [local(): lax.psum(jnp.concatenate(partial_q + [vector_total.reshape(rank, -1)], ax...]
    mul x6 -> x0, other arithmetic: 74.2 us -> none  [orthonormal(): column = column * lax.rsqrt(jnp.sum(column * column) + NORM_EPS)]
    all_gather x4 -> x1, blocking collectives: 30.8 us -> 9.3 us  [local(): whole_p = lax.all_gather(reduced, 'seq', axis=0, tiled=False)]
    dot_general x12 -> x8, matrix products: 39.2 us -> 28.1 us  [contract_cols(): lax.dot_general(left, right, (((1,), (1,)), ((), ())), precision=precisio...]
  transfers between devices with their start and end apart: 18 -> 17, of which waited for: 11 -> 10; matrix products, arithmetic and copies ran while one was open for 29% -> 38% of each run, Pallas kernels for 0% -> 0%
where the time goes in v1:
time: 1010 us; the launch traced here: 997 us
  waiting for transfers between devices  433 us (43%)
  matrix products  313 us (31%)
  blocking collectives  102 us (10%)
  local copies, waits for them, and re-layouts  66.9 us (7%)
  other arithmetic  62.4 us (6%)
  between operations  15.6 us (2%)
    psum x1, waiting for transfers between devices, local(): lax.psum(jnp.concatenate(partial_q + [vector_total.reshape(rank, -1)], ax...  120 us
    dot_general x2, matrix products, run_layer(): jnp.einsum('bhqk,bkhd->bqhd', grad_scores, key_heads, preferred_element_t...  65.8 us
    dot_general x2, matrix products, run_layer(): jnp.einsum('bhqk,bqhd->bkhd', grad_scores, query_heads, preferred_element...  59.9 us
    reduce_scatter x1, waiting for transfers between devices, local(): lax.psum_scatter(local_grads[2].astype(jnp.bfloat16), 'seq', scatter_dime...  55.1 us
    all_gather x1, waiting for transfers between devices, local(): lax.all_gather(widened[3], 'seq', axis=0, tiled=True)  53.5 us
    all_gather x1, waiting for transfers between devices, local(): lax.all_gather(widened[0], 'seq', axis=0, tiled=True)  46.9 us
    reduce_scatter x1, waiting for transfers between devices, local(): lax.psum_scatter(local_grads[3].astype(jnp.bfloat16), 'seq', scatter_dime...  44.2 us
    dot_general x8, matrix products, contract_rows(): lax.dot_general(left, right, (((0,), (0,)), ((), ())), precision=precisio...  40.1 us
  transfers between devices with their start and end apart: 17, of which 10 were waited for; matrix products, arithmetic and copies ran while one was open for 38% of the time, Pallas kernels for 0%

profile of v1, /device:TPU:0, one launch (start us, length us, event | category | flops | bytes accessed | tf_op | source)
XLA Modules:
  0.0 997.5 jit_solution(4652829139128204997)
XLA Ops:
  11.8 24.7 %all_gather.42 = bf16[192,2304]{0,1:T(8,128)(2,1)S(1)} all-gather(bf16[192,288]{0,1:T(8,128)(2,1)S(1)} %copy.125), channel_id=1, replica_groups=mesh['seq'=4,'rep'=8] {'rep'}, dimensions={1}, use_global_device_ids=true | all-gather | bytes 995328 | tf_op jit(solution)/shard_map/all_gather | solution.py:257
  38.0 14.4 %all_gather.46 = bf16[192,768]{0,1:T(8,128)(2,1)S(1)} all-gather(bf16[192,96]{0,1:T(8,128)(2,1)S(1)} %copy.132), channel_id=1, replica_groups=mesh['seq'=4,'rep'=8] {'rep'}, dimensions={1}, use_global_device_ids=true | all-gather | bytes 331776 | tf_op jit(solution)/shard_map/all_gather | solution.py:258
  54.0 10.9 %all-gather.23.cloned.1.call-done = bf16[768,768]{0,1:T(8,128)(2,1)} async-done(((bf16[768,96]{0,1:T(8,128)(2,1)}), bf16[768,768]{0,1:T(8,128)(2,1)}) %all-gather.23.cloned.1.call-update) | async-done | bytes 1179664 | tf_op jit(solution)/shard_map/all_gather | solution.py:260
  67.2 46.9 %all-gather.11.cloned.1.call-done = bf16[768,2304]{1,0:T(8,128)(2,1)} async-done(((bf16[192,2304]{1,0:T(8,128)(2,1)}), bf16[768,2304]{1,0:T(8,128)(2,1)}) %all-gather.11.cloned.1.call-update) | async-done | bytes 3538960 | tf_op jit(solution)/shard_map/all_gather | solution.py:263
  126.8 11.9 %all-gather.1 = bf16[512,768]{1,0:T(8,128)(2,1)S(1)} all-gather(bf16[128,768]{1,0:T(8,128)(2,1)S(1)} %slice.183), channel_id=3, replica_groups=mesh['seq'=4,'rep'=8] {'seq'}, dimensions={0}, use_global_device_ids=true | all-gather | bytes 983040 | tf_op jit(solution)/shard_map/all_gather | solution.py:115
  139.9 11.4 %all-gather = bf16[512,768]{1,0:T(8,128)(2,1)S(1)} all-gather(bf16[128,768]{1,0:T(8,128)(2,1)S(1)} %get-tuple-element.62), channel_id=2, replica_groups=mesh['seq'=4,'rep'=8] {'seq'}, dimensions={0}, use_global_device_ids=true | all-gather | bytes 983040 | tf_op jit(solution)/shard_map/all_gather | solution.py:116
  165.6 38.8 %all-gather.21.cloned.1.call-done = bf16[768,3072]{1,0:T(8,128)(2,1)} async-done(((bf16[192,3072]{1,0:T(8,128)(2,1)}), bf16[768,3072]{1,0:T(8,128)(2,1)}) %all-gather.21.cloned.1.call-update) | async-done | bytes 4718608 | tf_op jit(solution)/shard_map/all_gather | solution.py:265
  209.6 53.5 %all-gather.25.cloned.1.call-done = bf16[3072,768]{0,1:T(8,128)(2,1)} async-done(((bf16[768,768]{0,1:T(8,128)(2,1)}), bf16[3072,768]{0,1:T(8,128)(2,1)}) %all-gather.25.cloned.1.call-update) | async-done | bytes 4718608 | tf_op jit(solution)/shard_map/all_gather | solution.py:266
  286.6 12.9 %fusion.45 = f32[12,64,512]{2,1,0:T(8,128)} fusion(bf16[128,12,64]{0,2,1:T(8,128)(2,1)} %bitcast.287, f32[12,128,512]{2,1,0:T(8,128)} %fusion.217, f32[12,128,512]{2,1,0:T(8,128)S(1)} %get-tuple-element.86, f32[12,128]{1,0:T(8,128)S(1)} %log_add_fusion.1), kind=kOutput, calls=%fused_computation.57 | convolution fusion | flops 106170368 | bytes 8067072 | tf_op jit(solution)/shard_map/bhqk,bqhd->bkhd/dot_general | solution.py:178
  299.7 9.1 all-gather.15.cloned.1.call-done
  313.5 14.7 %fusion.4 = (f32[2,12,256]{2,1,0:T(8,128)S(1)}, f32[2,12,256,1024]{3,2,1,0:T(8,128)}) fusion(pred[256,1024]{1,0:T(8,128)(4,1)S(1)} %iota_compare_fusion, bf16[2,1024,12,64]{1,3,2,0:T(8,128)(2,1)} %bitcast.262, bf16[2,256,12,64]{1,0,3,2:T(2,128)(2,1)} %reshape.433), kind=kOutput, calls=%fused_computation.10 | convolution fusion | flops 824174592 | bytes 29384704 | tf_op jit(solution)/shard_map/bqhd,bkhd->bhqk/dot_general | solution.py:125
  328.3 12.4 %fusion.3 = f32[2,12,256]{2,1,0:T(8,128)} fusion(f32[2,12,256,1024]{3,2,1,0:T(8,128)} %get-tuple-element.82, f32[2,12,256]{2,1,0:T(8,128)S(1)} %get-tuple-element.81, pred[256,1024]{1,0:T(8,128)(4,1)S(1)} %iota_compare_fusion), kind=kLoop, calls=%fused_computation.9 | loop fusion | flops 25159680 | bytes 25477120 | tf_op jit(solution)/shard_map/reduce_sum | solution.py:133
  340.7 14.5 %all-gather.13.cloned.1.call-done = bf16[2,1024,768]{2,1,0:T(8,128)(2,1)} async-done(((bf16[2,256,768]{2,1,0:T(8,128)(2,1)}), bf16[2,1024,768]{2,1,0:T(8,128)(2,1)}) %all-gather.13.cloned.1.call-update) | async-done | bytes 3145744 | tf_op jit(solution)/shard_map/all_gather | solution.py:116
  359.8 12.9 %fusion.87 = bf16[2,256,12,64]{1,3,2,0:T(8,128)(2,1)S(1)} fusion(bf16[2,1024,12,64]{1,3,2,0:T(8,128)(2,1)} %bitcast.258, f32[2,12,256,1024]{3,2,1,0:T(8,128)} %get-tuple-element.82, f32[2,12,256]{2,1,0:T(8,128)} %fusion.3, f32[2,12,256]{2,1,0:T(8,128)S(1)} %get-tuple-element.81, pred[256,1024]{1,0:T(8,128)(4,1)S(1)} %iota_compare_fusion), kind=kOutput, calls=%fused_computation.123 | convolution fusion | flops 837156864 | bytes 29409280 | tf_op jit(solution)/shard_map/bhqk,bkhd->bqhd/dot_general | solution.py:137
  379.7 8.6 fusion.198
  403.2 14.2 %fusion.5 = f32[2,12,64,1024]{3,2,1,0:T(8,128)} fusion(f32[2,12,256,1024]{3,2,1,0:T(8,128)} %get-tuple-element.82, f32[2,12,256]{2,1,0:T(8,128)S(1)} %log_add_fusion, pred[256,1024]{1,0:T(8,128)(4,1)S(1)} %iota_compare_fusion, bf16[2,256,12,64]{1,0,3,2:T(2,128)(2,1)} %reshape.447), kind=kOutput, calls=%fused_computation.11 | convolution fusion | flops 830472192 | bytes 32530432 | tf_op jit(solution)/shard_map/bhqk,bqhd->bkhd/dot_general | solution.py:167
  417.4 6.6 copy.143
  424.1 14.9 %fusion.111 = f32[2,12,256,1024]{3,2,1,0:T(8,128)} fusion(bf16[2,1024,12,64]{1,3,2,0:T(8,128)(2,1)} %bitcast.259, bf16[2,256,12,64]{1,0,3,2:T(2,128)(2,1)} %reshape.447), kind=kOutput, calls=%fused_computation.155 | convolution fusion | flops 805306368 | bytes 29097984 | tf_op jit(solution)/shard_map/bqhd,bkhd->bhqk/dot_general | solution.py:170
  439.0 47.0 %fusion.11 = f32[2,12,64,1024]{3,2,1,0:T(8,128)} fusion(f32[2,12,256,1024]{3,2,1,0:T(8,128)} %fusion.111, f32[2,12,256,1024]{3,2,1,0:T(8,128)} %get-tuple-element.82, f32[2,12,256]{2,1,0:T(8,128)S(1)} %copy-done.75, pred[256,1024]{1,0:T(8,128)(4,1)S(1)} %iota_compare_fusion, bf16[2,256,12,64]{1,0,3,2:T(2,128)(2,1)} %reshape.433), kind=kOutput, calls=%fused_computation.14 | convolution fusion | flops 874519552 | bytes 57696256 | tf_op jit(solution)/shard_map/bhqk,bqhd->bkhd/dot_general | solution.py:178
  486.0 6.6 copy.141
  496.7 8.5 convolution_convert_fusion
  505.2 9.2 convolution_convert_fusion.1
  514.5 13.5 %fusion.205 = (f32[12,64]{1,0:T(8,128)}, bf16[1,128,12,64]{1,3,2,0:T(8,128)(2,1)}) fusion(bf16[512,12,64]{0,2,1:T(8,128)(2,1)} %bitcast.272, f32[12,128,512]{2,1,0:T(8,128)} %fusion.217, f32[12,128,512]{2,1,0:T(8,128)S(1)} %get-tuple-element.86, f32[12,128]{1,0:T(8,128)S(1)} %log_add_fusion.1), kind=kOutput, calls=%fused_computation.326 | convolution fusion | flops 106366208 | bytes 7283712 | tf_op jit(solution)/shard_map/bhqk,bkhd->bqhd/dot_general | solution.py:175
  528.0 52.3 %bitcast_convert_fusion = (bf16[2,256,12,64]{1,3,2,0:T(8,128)(2,1)S(1)}, f32[2,12,64,256]{3,2,1,0:T(8,128)}) fusion(bf16[2,1024,12,64]{1,3,2,0:T(8,128)(2,1)} %bitcast.263, f32[2,12,256,1024]{3,2,1,0:T(8,128)} %fusion.111, f32[2,12,256]{2,1,0:T(8,128)S(1)} %copy-done.75, f32[2,12,256,1024]{3,2,1,0:T(8,128)} %get-tuple-element.82, ...), kind=kOutput, calls=%fused_computation.88 | convolution fusion | flops 874912768 | bytes 56123392 | tf_op jit(solution)/shard_map/bhqk,bkhd->bqhd/dot_general | solution.py:175
  591.3 6.1 convolution_convert_fusion.2
  605.4 7.2 add_add_fusion.4
  617.9 44.2 %reduce-scatter.23.cloned.1.call-done = bf16[768,768]{1,0:T(8,128)(2,1)} async-done(((bf16[3072,768]{1,0:T(8,128)(2,1)}), bf16[768,768]{1,0:T(8,128)(2,1)}) %reduce-scatter.23.cloned.1.call-update) | async-done | bytes 1179664 | tf_op jit(solution)/shard_map/reduce_scatter | solution.py:307
  666.8 55.1 %reduce-scatter.21.cloned.1.call-done = bf16[192,3072]{1,0:T(8,128)(2,1)} async-done(((bf16[768,3072]{1,0:T(8,128)(2,1)}), bf16[192,3072]{1,0:T(8,128)(2,1)}) %reduce-scatter.21.cloned.1.call-update) | async-done | bytes 1179664 | tf_op jit(solution)/shard_map/reduce_scatter | solution.py:304
  733.5 38.5 %reduce-scatter.17.cloned.1.call-done = bf16[192,2304]{1,0:T(8,128)(2,1)} async-done(((bf16[768,2304]{1,0:T(8,128)(2,1)}), bf16[192,2304]{1,0:T(8,128)(2,1)}) %reduce-scatter.17.cloned.1.call-update) | async-done | bytes 884752 | tf_op jit(solution)/shard_map/reduce_scatter | solution.py:298
  776.7 30.0 %psum.14 = f32[1,8,1536]{2,1,0:T(8,128)} all-reduce(f32[1,8,1536]{2,1,0:T(8,128)} %fusion.143), channel_id=1, replica_groups=mesh['seq'=4,'rep'=8] {'rep'}, use_global_device_ids=true, to_apply=%region_33.34 | all-reduce | flops 12288 | bytes 98304 | tf_op jit(solution)/shard_map/psum | solution.py:333
  806.7 9.3 all_gather.55.p_ref
  833.3 119.9 %all-reduce.5.cloned.1.call-done = f32[8,8064]{1,0:T(8,128)} async-done(((f32[8,8064]{1,0:T(8,128)}), f32[8,8064]{1,0:T(8,128)}) %all-reduce.5.cloned.1.call-update) | async-done | bytes 258064 | tf_op jit(solution)/shard_map/psum | solution.py:351
  (426 shorter events, 200.8 us)
Async XLA Ops:
  7.2 714.7 %copy-start = (f32[3072,8]{0,1:T(8,128)S(1)}, f32[3072,8]{0,1:T(8,128)}, u32[]{:S(2)}) copy-start(f32[3072,8]{0,1:T(8,128)} %param.42) | copy-start | bytes 294916
  7.2 46.2 %all-gather.19.cloned.1.call-start = ((), (), s32[]{:S(2)}) async-start(), calls=%async_computation.12 | async-start | bytes 1327104 | tf_op jit(solution)/shard_map/all_gather | solution.py:259
  9.0 55.9 %all-gather.23.cloned.1.call-start = ((), (), s32[]{:S(2)}) async-start(), calls=%async_computation.14 | async-start | bytes 1327104 | tf_op jit(solution)/shard_map/all_gather | solution.py:260
  10.7 103.4 %all-gather.11.cloned.1.call-start = ((), (), s32[]{:S(2)}) async-start(), calls=%async_computation.8 | async-start | bytes 4423680 | tf_op jit(solution)/shard_map/all_gather | solution.py:263
  37.8 124.3 %all-gather.17.cloned.1.call-start = ((), (), s32[]{:S(2)}) async-start(), calls=%async_computation.11 | async-start | bytes 1474560 | tf_op jit(solution)/shard_map/all_gather | solution.py:264
  53.3 151.1 %all-gather.21.cloned.1.call-start = ((), (), s32[]{:S(2)}) async-start(), calls=%async_computation.13 | async-start | bytes 5898240 | tf_op jit(solution)/shard_map/all_gather | solution.py:265
  53.9 209.2 %all-gather.25.cloned.1.call-start = ((), (), s32[]{:S(2)}) async-start(), calls=%async_computation.15 | async-start | bytes 5898240 | tf_op jit(solution)/shard_map/all_gather | solution.py:266
  64.9 243.9 %all-gather.15.cloned.1.call-start = ((), (), s32[]{:S(2)}) async-start(), calls=%async_computation.10 | async-start | bytes 3932160 | tf_op jit(solution)/shard_map/all_gather | solution.py:115
  65.2 53.0 %copy-start.70 = (f32[1,2,2,128]{3,1,2,0:T(2,128)}, f32[1,2,2,128]{3,1,2,0:T(2,128)S(1)}, u32[]{:S(2)}) copy-start(f32[1,2,2,128]{3,1,2,0:T(2,128)S(1)} %copy.148) | copy-start | bytes 6148
  66.2 52.0 %copy-start.72 = (f32[512]{0:T(512)}, f32[512]{0:T(512)S(1)}, u32[]{:S(2)}) copy-start(f32[512]{0:T(512)S(1)} %rsqrt.40) | copy-start | bytes 6148
  66.8 56.0 %copy-start.60 = (f32[768]{0:T(1024)}, f32[768]{0:T(1024)S(1)}, u32[]{:S(2)}) copy-start(f32[768]{0:T(1024)S(1)} %get-tuple-element.78) | copy-start | bytes 9220
  66.8 95.4 %copy-start.81 = (f32[768]{0:T(1024)}, f32[768]{0:T(1024)S(1)}, u32[]{:S(2)}) copy-start(f32[768]{0:T(1024)S(1)} %get-tuple-element.74) | copy-start | bytes 9220
  67.1 51.0 %copy-start.48 = (bf16[512,768]{1,0:T(8,128)(2,1)}, bf16[512,768]{1,0:T(8,128)(2,1)S(1)}, u32[]{:S(2)}) copy-start(bf16[512,768]{1,0:T(8,128)(2,1)S(1)} %fusion.72) | copy-start | bytes 2359300
  67.1 54.8 %copy-start.106 = (s32[1,4]{1,0:T(1,128)S(1)}, s32[1,4]{1,0:T(1,128)}, u32[]{:S(2)}) copy-start(s32[1,4]{1,0:T(1,128)} %param.27) | copy-start | bytes 52
  67.2 55.1 %copy-start.25 = (bf16[1,128,768]{2,1,0:T(8,128)(2,1)S(1)}, bf16[1,128,768]{2,1,0:T(8,128)(2,1)}, u32[]{:S(2)}) copy-start(bf16[1,128,768]{2,1,0:T(8,128)(2,1)} %param.24) | copy-start | bytes 589828
  121.3 233.9 %all-gather.13.cloned.1.call-start = ((), (), s32[]{:S(2)}) async-start(), calls=%async_computation.9 | async-start | bytes 3932160 | tf_op jit(solution)/shard_map/all_gather | solution.py:116
  158.9 422.4 %reduce-scatter.15.cloned.1.call-start = ((), (), s32[]{:S(2)}) async-start(), calls=%async_computation.19 | async-start | bytes 1966080 | tf_op jit(solution)/shard_map/reduce_scatter | solution.py:185
  165.6 97.5 %copy-start.41 = (bf16[1,128,768]{2,1,0:T(8,128)(2,1)S(1)}, bf16[1,128,768]{2,1,0:T(8,128)(2,1)}, u32[]{:S(2)}) copy-start(bf16[1,128,768]{2,1,0:T(8,128)(2,1)} %param.26) | copy-start | bytes 589828
  277.5 305.9 %reduce-scatter.13.cloned.1.call-start = ((), (), s32[]{:S(2)}) async-start(), calls=%async_computation.18 | async-start | bytes 1966080 | tf_op jit(solution)/shard_map/reduce_scatter | solution.py:182
  299.5 285.7 %reduce-scatter.11.cloned.1.call-start = ((), (), s32[]{:S(2)}) async-start(), calls=%async_computation.17 | async-start | bytes 7864320 | tf_op jit(solution)/shard_map/reduce_scatter | solution.py:185
  424.0 164.3 %reduce-scatter.9.cloned.1.call-start = ((), (), s32[]{:S(2)}) async-start(), calls=%async_computation.16 | async-start | bytes 7864320 | tf_op jit(solution)/shard_map/reduce_scatter | solution.py:182
  492.6 123.1 %reduce-scatter.19.cloned.1.call-start = ((), (), s32[]{:S(2)}) async-start(), calls=%async_computation.21 | async-start | bytes 1474560 | tf_op jit(solution)/shard_map/reduce_scatter | solution.py:301
  496.6 165.5 %reduce-scatter.23.cloned.1.call-start = ((), (), s32[]{:S(2)}) async-start(), calls=%async_computation.23 | async-start | bytes 5898240 | tf_op jit(solution)/shard_map/reduce_scatter | solution.py:307
  505.2 216.8 %reduce-scatter.21.cloned.1.call-start = ((), (), s32[]{:S(2)}) async-start(), calls=%async_computation.22 | async-start | bytes 5898240 | tf_op jit(solution)/shard_map/reduce_scatter | solution.py:304
  514.4 257.6 %reduce-scatter.17.cloned.1.call-start = ((), (), s32[]{:S(2)}) async-start(), calls=%async_computation.20 | async-start | bytes 4423680 | tf_op jit(solution)/shard_map/reduce_scatter | solution.py:298
  597.5 355.7 %all-reduce.5.cloned.1.call-start = ((), (), s32[]{:S(2)}) async-start(), calls=%async_computation.24 | async-start | bytes 516096 | tf_op jit(solution)/shard_map/psum | solution.py:351
  612.8 49.3 %copy-start.76 = (f32[768,8]{0,1:T(8,128)S(1)}, f32[768,8]{0,1:T(8,128)}, u32[]{:S(2)}) copy-start(f32[768,8]{0,1:T(8,128)} %param.43) | copy-start | bytes 73732
  614.6 107.4 %copy-start.1 = (f32[1,192,3072]{2,1,0:T(8,128)S(1)}, f32[1,192,3072]{2,1,0:T(8,128)}, u32[]{:S(2)}) copy-start(f32[1,192,3072]{2,1,0:T(8,128)} %param.38) | copy-start | bytes 7077892
  617.9 108.0 %copy-start.6 = (bf16[1,2,256,768]{3,2,1,0:T(8,128)(2,1)S(1)}, bf16[1,2,256,768]{3,2,1,0:T(8,128)(2,1)}, u32[]{:S(2)}) copy-start(bf16[1,2,256,768]{3,2,1,0:T(8,128)(2,1)} %param.23) | copy-start | bytes 2359300
  617.9 108.0 %copy-start.71 = (f32[1,2,2,128]{3,1,2,0:T(2,128)S(1)}, f32[1,2,2,128]{3,1,2,0:T(2,128)}, u32[]{:S(2)}) copy-start(f32[1,2,2,128]{3,1,2,0:T(2,128)} %copy-done.70) | copy-start | bytes 6148
  733.5 90.2 %copy-start.39 = (bf16[192,768]{1,0:T(8,128)(2,1)S(1)}, bf16[192,768]{1,0:T(8,128)(2,1)}, u32[]{:S(2)}) copy-start(bf16[192,768]{1,0:T(8,128)(2,1)} %reduce-scatter.19.cloned.1.call-done) | copy-start | bytes 884740
  833.3 128.5 %copy-start.57 = (f32[8,1536]{1,0:T(8,128)S(1)}, f32[8,1536]{1,0:T(8,128)}, u32[]{:S(2)}) copy-start(f32[8,1536]{1,0:T(8,128)} %copy-done.56) | copy-start | bytes 147460
  (98 other events, 556.8 us)
Sparse Core Ops, SparseCore 0:
  10.2 30.0 all-gather.18
  42.6 22.2 all-gather.22
  67.3 46.7 all-gather.10
  116.4 29.3 all-gather.16
  147.5 56.9 all-gather.20
  206.1 56.9 all-gather.24
  265.0 43.8 all-gather.14
  311.2 43.8 all-gather.12
  358.7 31.1 reduce-scatter.14
  393.3 31.1 reduce-scatter.12
  427.5 70.0 reduce-scatter.10
  500.4 70.1 reduce-scatter.8
  573.5 28.6 reduce-scatter.18
  605.1 56.9 reduce-scatter.22
  664.9 56.9 reduce-scatter.20
  724.9 47.1 reduce-scatter.16
  829.4 123.7 all-reduce.4

commit v2 on v1

v2 whole, which is shorter than its diff:
```python
from functools import partial

import jax
import jax.numpy as jnp
from jax import lax
from jax.experimental import pallas as pl
from jax.experimental.pallas import tpu as pltpu
from jax.sharding import PartitionSpec as P

D = 768
HEADS = 12
HDIM = 64
LANES = 128


LN_EPS = 1e-05
NORM_EPS = 1e-06
BETA = 0.9
RATE_MATRIX = 0.1
RATE_VECTOR = 0.01
MASKED = -1e30
HIGH = lax.Precision.HIGHEST


def layer_norm(values, gain, shift):
    center = values - jnp.mean(values, axis=-1, keepdims=True)
    spread = jnp.mean(center * center, axis=-1, keepdims=True)
    return center * lax.rsqrt(spread + LN_EPS) * gain + shift


def unpack(vectors):
    head = vectors[: 8 * D].reshape(8, D)
    return (
        head[0],
        head[1],
        head[2],
        head[3],
        head[4],
        head[5],
        head[6],
        head[7],
        vectors[8 * D :],
    )


def orthonormal(gathered, widths, scale):
    rank = gathered.shape[1]

    def over_pieces(values):
        parts = [values[at : at + 1] for at in range(values.shape[0])]
        while len(parts) > 1:
            parts = [left + right for left, right in zip(parts[::2], parts[1::2])]
        return parts[0]

    def kernel(p_ref, basis_ref):
        offset = 0
        for width in widths:
            block = p_ref[:, :, offset : offset + width] * scale
            row_ids = lax.broadcasted_iota(jnp.int32, (1, rank, 1), 1)
            for column_id in range(rank):
                column = block[:, column_id : column_id + 1, :]
                length = over_pieces(jnp.sum(column * column, axis=2, keepdims=True))
                unit = column * lax.rsqrt(length + NORM_EPS)
                inner = over_pieces(jnp.sum(block * unit, axis=2, keepdims=True))
                later = jnp.where(row_ids > column_id, inner, 0.0)
                block = jnp.where(row_ids == column_id, unit, block - later * unit)
            basis_ref[:, offset : offset + width] = block[0]
            offset += width

    return pl.pallas_call(
        kernel, out_shape=jax.ShapeDtypeStruct(gathered.shape[1:], jnp.float32), name="orthonormal"
    )(gathered)


def contract_rows(left, right, precision=None):
    return lax.dot_general(
        left,
        right,
        (((0,), (0,)), ((), ())),
        precision=precision,
        preferred_element_type=jnp.float32,
    )


def contract_cols(left, right, precision=None):
    return lax.dot_general(
        left,
        right,
        (((1,), (1,)), ((), ())),
        precision=precision,
        preferred_element_type=jnp.float32,
    )


def swap_with(values, axis, distance):
    count = lax.axis_size(axis)
    return lax.ppermute(values, axis, [(source, source ^ distance) for source in range(count)])


def butterfly_sum(values, axis):
    distance = 1
    while distance < lax.axis_size(axis):
        values = values + swap_with(values, axis, distance)
        distance *= 2
    return values


def gather_stacked(values, axis):
    count = lax.axis_size(axis)
    return jnp.stack(
        [values] + [swap_with(values, axis, distance) for distance in range(1, count)]
    )


def halve(blocks, axis_at, distance):
    bit = (lax.axis_index("seq") // distance) % 2
    sent = lax.dynamic_index_in_dim(blocks, 1 - bit, axis_at, keepdims=False)
    kept = lax.dynamic_index_in_dim(blocks, bit, axis_at, keepdims=False)
    received = swap_with(sent, "seq", distance)
    return kept.astype(jnp.float32) + received.astype(jnp.float32)


def scatter_rows(matrix):
    rows, columns = matrix.shape
    if lax.axis_size("seq") != 4:
        return lax.psum_scatter(matrix, "seq", scatter_dimension=0, tiled=True).astype(jnp.float32)
    blocks = matrix.reshape(2, 2, rows // 4, columns)
    middle = columns // 2
    first = halve(blocks[..., :middle], 1, 1).astype(jnp.bfloat16)
    second = halve(blocks[..., middle:], 0, 2).astype(jnp.bfloat16)
    return jnp.concatenate([halve(first, 0, 2), halve(second, 0, 1)], axis=1)


def exchange(values):
    return lax.all_to_all(values, "seq", split_axis=0, concat_axis=0, tiled=True)


def dot_of(left, right, left_dim, right_dim):
    return lax.dot_general(
        left,
        right,
        (((left_dim,), (right_dim,)), ((), ())),
        preferred_element_type=jnp.float32,
    )


def attention_calls(chunks, batch, length, short_length, width, dtype=jnp.bfloat16):
    heads = width // HDIM
    scale = HDIM ** (-0.5)
    rows_all = batch * length + short_length
    smem = pl.BlockSpec(memory_space=pltpu.SMEM)
    vmem = pl.BlockSpec(memory_space=pltpu.VMEM)

    def causal(size):
        key_ids = lax.broadcasted_iota(jnp.int32, (size, size), 0)
        query_ids = lax.broadcasted_iota(jnp.int32, (size, size), 1)
        return key_ids <= query_ids

    def long_mask(scores, key_at, query_at):
        if key_at != query_at:
            return scores
        return jnp.where(causal(length), scores, MASKED)

    def short_mask_of(docs_ref):
        ends = []
        end = 0
        for number in range(docs_ref.shape[1]):
            end = end + docs_ref[0, number]
            ends.append(end)

        def document(position):
            found = jnp.zeros_like(position)
            for end in ends:
                found = found + jnp.where(position >= end, 1, 0)
            return found

        def short_mask(scores, key_at, query_at):
            size = short_length
            key_ids = lax.broadcasted_iota(jnp.int32, (size, 1), 0) + key_at * size
            query_ids = lax.broadcasted_iota(jnp.int32, (1, size), 1) + query_at * size
            allowed = document(key_ids) == document(query_ids)
            if key_at == query_at:
                allowed = allowed & causal(size)
            return jnp.where(allowed, scores, MASKED)

        return short_mask

    def parts_of(ref, first, size, start, head):
        low = start + head * HDIM
        return [ref[chunk, pl.ds(first, size), low : low + HDIM] for chunk in range(chunks)]

    def forward(docs_ref, joined_ref, mixed_ref, long_log_ref, short_log_ref):
        def run(first, size, mask, log_store):
            for query_at in range(chunks):
                pieces = []
                for head in range(heads):
                    low = head * HDIM
                    query = joined_ref[query_at, pl.ds(first, size), low : low + HDIM] * scale
                    keys = parts_of(joined_ref, first, size, width, head)
                    values = parts_of(joined_ref, first, size, 2 * width, head)
                    scores = [
                        mask(dot_of(keys[at], query, 1, 1), at, query_at)
                        for at in range(query_at + 1)
                    ]
                    top = jnp.max(scores[0], axis=0, keepdims=True)
                    for part in scores[1:]:
                        top = jnp.maximum(top, jnp.max(part, axis=0, keepdims=True))
                    expo = [jnp.exp(part - top) for part in scores]
                    total = sum(jnp.sum(part, axis=0, keepdims=True) for part in expo)
                    inverse = 1.0 / total
                    pieces.append(
                        sum(
                            dot_of(values[at], (expo[at] * inverse).astype(dtype), 0, 0)
                            for at in range(query_at + 1)
                        )
                    )
                    log_store(query_at, head, top + jnp.log(total))
                mixed = jnp.concatenate(pieces, axis=0).T
                mixed_ref[query_at, pl.ds(first, size), :] = mixed.astype(dtype)

        def long_step(number, carry):
            def store(query_at, head, log_total):
                long_log_ref[number, query_at, head : head + 1, :] = log_total

            run(pl.multiple_of(number * length, length), length, long_mask, store)
            return carry

        lax.fori_loop(0, batch, long_step, 0)

        def short_store(query_at, head, log_total):
            short_log_ref[query_at, head : head + 1, :] = log_total

        run(batch * length, short_length, short_mask_of(docs_ref), short_store)

    def backward(
        docs_ref, joined_ref, grad_ref, long_log_ref, short_log_ref, out_ref, sums_ref
    ):
        sums_ref[...] = jnp.zeros_like(sums_ref)

        def run(first, size, mask, log_load):
            grad_query = [[] for _ in range(chunks)]
            grad_key = [[] for _ in range(chunks)]
            grad_value = [[] for _ in range(chunks)]
            for head in range(heads):
                keys = parts_of(joined_ref, first, size, width, head)
                values = parts_of(joined_ref, first, size, 2 * width, head)
                queries = parts_of(joined_ref, first, size, 0, head)
                grads = parts_of(grad_ref, first, size, 0, head)
                key_sums = [0.0] * chunks
                value_sums = [0.0] * chunks
                for query_at in range(chunks):
                    query = queries[query_at] * scale
                    grad = grads[query_at]
                    log_total = log_load(query_at, head)
                    soft = []
                    soft_grad = []
                    inner = 0.0
                    for at in range(query_at + 1):
                        scores = mask(dot_of(keys[at], query, 1, 1), at, query_at)
                        soft.append(jnp.exp(scores - log_total))
                        soft_grad.append(dot_of(values[at], grad, 1, 1))
                        inner = inner + jnp.sum(soft[at] * soft_grad[at], axis=0, keepdims=True)
                    query_sum = 0.0
                    for at in range(query_at + 1):
                        score_grad = (soft[at] * (soft_grad[at] - inner)).astype(dtype)
                        query_sum = query_sum + dot_of(keys[at], score_grad, 0, 0)
                        key_sums[at] = key_sums[at] + dot_of(score_grad, query, 1, 0)
                        value_sums[at] = value_sums[at] + dot_of(
                            soft[at].astype(dtype), grad, 1, 0
                        )
                    grad_query[query_at].append(query_sum * scale)
                for at in range(chunks):
                    grad_key[at].append(key_sums[at])
                    grad_value[at].append(value_sums[at])
            for at in range(chunks):
                query_all = jnp.concatenate(grad_query[at], axis=0).T
                value_all = jnp.concatenate(grad_value[at], axis=1)
                sums_ref[0:1, :] += jnp.sum(query_all, axis=0, keepdims=True)
                sums_ref[1:2, :] += jnp.sum(value_all, axis=0, keepdims=True)
                out_ref[at, pl.ds(first, size), :] = jnp.concatenate(
                    [query_all] + grad_key[at] + [value_all], axis=1
                ).astype(dtype)

        def long_step(number, carry):
            def load(query_at, head):
                return long_log_ref[number, query_at, head : head + 1, :]

            run(pl.multiple_of(number * length, length), length, long_mask, load)
            return carry

        lax.fori_loop(0, batch, long_step, 0)

        def short_load(query_at, head):
            return short_log_ref[query_at, head : head + 1, :]

        run(batch * length, short_length, short_mask_of(docs_ref), short_load)

    forward_call = pl.pallas_call(
        forward,
        out_shape=(
            jax.ShapeDtypeStruct((chunks, rows_all, width), dtype),
            jax.ShapeDtypeStruct((batch, chunks, heads, length), jnp.float32),
            jax.ShapeDtypeStruct((chunks, heads, short_length), jnp.float32),
        ),
        in_specs=[smem, vmem],
        out_specs=(vmem, vmem, vmem),
        name="attention_forward",
    )
    backward_call = pl.pallas_call(
        backward,
        out_shape=(
            jax.ShapeDtypeStruct((chunks, rows_all, 3 * width), dtype),
            jax.ShapeDtypeStruct((2, width), jnp.float32),
        ),
        in_specs=[smem, vmem, vmem, vmem, vmem],
        out_specs=(vmem, vmem),
        name="attention_backward",
    )
    return forward_call, backward_call


def run_layer(tokens, cotangent, docs, batch, length, weights, vectors):
    w_attend, w_merge, w_expand, w_contract = weights
    (
        gain_one,
        shift_one,
        bias_query,
        bias_value,
        bias_merge,
        gain_two,
        shift_two,
        bias_contract,
        bias_expand,
    ) = unpack(vectors)
    rows_all = tokens.shape[0]
    chunks = lax.axis_size("seq")
    width = D // chunks
    forward_call, backward_call = attention_calls(
        chunks, batch, length, rows_all - batch * length, width
    )
    inputs = tokens.astype(jnp.float32)
    normed_one, norm_one_back = jax.vjp(layer_norm, inputs, gain_one, shift_one)
    normed_low = normed_one.astype(jnp.bfloat16)
    joined = jnp.dot(normed_low, w_attend, preferred_element_type=jnp.float32)
    joined_bias = jnp.concatenate([bias_query, jnp.zeros_like(bias_query), bias_value])
    joined_all = (joined + joined_bias).astype(jnp.bfloat16)
    by_heads = exchange(
        joined_all.reshape(rows_all, 3, chunks, width)
        .transpose(2, 0, 1, 3)
        .reshape(chunks, rows_all, 3 * width)
    )
    mixed_heads, long_log, short_log = forward_call(docs, by_heads)
    mixed = exchange(mixed_heads).transpose(1, 0, 2).reshape(rows_all, D)
    middle = inputs + jnp.dot(mixed, w_merge, preferred_element_type=jnp.float32) + bias_merge
    normed_two, norm_two_back = jax.vjp(layer_norm, middle, gain_two, shift_two)
    hidden = normed_two.astype(jnp.bfloat16)
    expanded = jnp.dot(hidden, w_expand, preferred_element_type=jnp.float32) + bias_expand
    activated, gelu_back = jax.vjp(partial(jax.nn.gelu, approximate=True), expanded)
    active_low = activated.astype(jnp.bfloat16)
    output = (
        middle + jnp.dot(active_low, w_contract, preferred_element_type=jnp.float32) + bias_contract
    )
    grad_out = cotangent.astype(jnp.float32)
    contract_bias_grad = jnp.sum(grad_out, axis=0)
    grad_active = contract_cols(cotangent, w_contract)
    (grad_expanded,) = gelu_back(grad_active)
    expand_bias_grad = jnp.sum(grad_expanded, axis=0)
    expanded_low = grad_expanded.astype(jnp.bfloat16)
    grad_hidden = contract_cols(expanded_low, w_expand)
    middle_part, gain_two_grad, shift_two_grad = norm_two_back(grad_hidden)
    grad_middle = grad_out + middle_part
    merge_bias_grad = jnp.sum(grad_middle, axis=0)
    middle_low = grad_middle.astype(jnp.bfloat16)
    grad_mixed = contract_cols(middle_low, w_merge).astype(jnp.bfloat16)
    grad_heads = exchange(grad_mixed.reshape(rows_all, chunks, width).transpose(1, 0, 2))
    joined_heads, head_sums = backward_call(docs, by_heads, grad_heads, long_log, short_log)
    joined_low = (
        exchange(joined_heads)
        .reshape(chunks, rows_all, 3, width)
        .transpose(1, 2, 0, 3)
        .reshape(rows_all, 3 * D)
    )
    bias_sums = lax.dynamic_update_slice_in_dim(
        jnp.zeros((2, D), jnp.float32), head_sums, lax.axis_index("seq") * width, 1
    )
    grad_normed = contract_cols(joined_low, w_attend)
    input_part, gain_one_grad, shift_one_grad = norm_one_back(grad_normed)
    grad_input = grad_middle + input_part
    vector_grad = jnp.concatenate(
        [
            gain_one_grad,
            shift_one_grad,
            bias_sums[0],
            bias_sums[1],
            merge_bias_grad,
            gain_two_grad,
            shift_two_grad,
            contract_bias_grad,
            expand_bias_grad,
        ]
    )
    operands = (
        normed_low,
        joined_low,
        mixed,
        middle_low,
        hidden,
        expanded_low,
        active_low,
        cotangent,
    )
    return output, grad_input, operands, vector_grad


def gather_weights(masters):
    attend, merge, expand, contract = (master.astype(jnp.bfloat16) for master in masters)
    rows = attend.shape[0]
    pieces = contract.shape[0] // rows
    packs = (
        jnp.concatenate([attend, merge], axis=1),
        expand,
        jnp.concatenate([contract[at * rows : (at + 1) * rows] for at in range(pieces)], axis=1),
    )
    seq_count = lax.axis_size("seq")
    rep_count = lax.axis_size("rep")
    whole = [
        lax.all_gather(pack, ("seq", "rep"), axis=0, tiled=False).reshape(
            seq_count, rep_count, rows, pack.shape[1]
        )
        for pack in packs
    ]

    def join(blocks):
        return blocks.transpose(0, 2, 1, 3).reshape(seq_count * rows, -1)

    split = attend.shape[1]
    contract_blocks = whole[2].reshape(seq_count, rep_count, rows, pieces, contract.shape[1])
    return (
        join(whole[0][..., :split]),
        join(whole[0][..., split:]),
        join(whole[1]),
        contract_blocks.transpose(0, 3, 2, 1, 4).reshape(seq_count * pieces * rows, -1),
    )


def local(
    long_input,
    short_input,
    long_cotangent,
    short_cotangent,
    doc_lengths,
    master_attend,
    master_merge,
    master_expand,
    master_contract,
    momentum_attend,
    momentum_merge,
    momentum_expand,
    momentum_contract,
    error_attend,
    error_merge,
    error_expand,
    error_contract,
    factor_attend,
    factor_merge,
    factor_expand,
    factor_contract,
    vector_params,
    vector_momentum,
):
    masters = (master_attend, master_merge, master_expand, master_contract)
    weights = gather_weights(masters)
    seq_index = lax.axis_index("seq")
    rep_index = lax.axis_index("rep")
    rep_count = lax.axis_size("rep")
    _, batch, length, _ = long_input.shape
    tokens = jnp.concatenate([long_input.reshape(-1, D), short_input[0]], axis=0)
    cotangent = jnp.concatenate([long_cotangent.reshape(-1, D), short_cotangent[0]], axis=0)
    output, grad_input, operands, vector_total = run_layer(
        tokens, cotangent, doc_lengths, batch, length, weights, vector_params
    )
    summed = [
        scatter_rows(
            contract_rows(operands[2 * number], operands[2 * number + 1]).astype(jnp.bfloat16)
        )
        for number in range(4)
    ]
    errors = (error_attend, error_merge, error_expand, error_contract)
    factors = (factor_attend, factor_merge, factor_expand, factor_contract)
    momenta = (momentum_attend, momentum_merge, momentum_expand, momentum_contract)
    corrected = [summed[number] + errors[number][0] for number in range(4)]
    heights = [corrected[number].shape[0] for number in range(4)]
    padded = [-(-height // LANES) * LANES for height in heights]
    projected = jnp.concatenate(
        [
            jnp.pad(
                lax.dot_general(
                    factors[number],
                    corrected[number],
                    (((0,), (1,)), ((), ())),
                    precision=HIGH,
                    preferred_element_type=jnp.float32,
                ),
                ((0, 0), (0, padded[number] - heights[number])),
            )
            for number in range(4)
        ],
        axis=1,
    )
    reduced = butterfly_sum(projected, "rep")
    whole_p = gather_stacked(reduced, "seq")
    basis_own = orthonormal(whole_p, padded, 1.0 / rep_count)
    basis_rows = []
    partial_q = []
    offset = 0
    for number in range(4):
        own_rows = basis_own[:, offset : offset + heights[number]]
        offset += padded[number]
        basis_rows.append(own_rows)
        partial_q.append(
            jnp.dot(
                own_rows, corrected[number], precision=HIGH, preferred_element_type=jnp.float32
            )
        )
    rank = projected.shape[0]
    renewed_all = jnp.concatenate(partial_q + [vector_total.reshape(rank, -1)], axis=1)
    renewed_all = butterfly_sum(butterfly_sum(renewed_all, "seq"), "rep")
    renewed_all = renewed_all / rep_count
    updated = []
    new_momenta = []
    new_errors = []
    new_factors = []
    offset = 0
    for number in range(4):
        columns = corrected[number].shape[1]
        renewed = renewed_all[:, offset : offset + columns]
        offset += columns
        approx = contract_rows(basis_rows[number], renewed, HIGH)
        new_errors.append((corrected[number] - approx)[None])
        width = masters[number].shape[1]
        own_block = lax.dynamic_slice_in_dim(approx, rep_index * width, width, 1)
        momentum_next = BETA * momenta[number] + own_block
        new_momenta.append(momentum_next)
        updated.append(masters[number] - RATE_MATRIX * momentum_next)
        new_factors.append(renewed.T)
    vector_grad = renewed_all[:, offset:].reshape(vector_total.shape)
    momenta_vectors = BETA * vector_momentum + vector_grad
    updated_vectors = vector_params - RATE_VECTOR * momenta_vectors
    split = batch * length
    long_output = output[:split].reshape(long_input.shape)
    long_grad = grad_input[:split].reshape(long_input.shape)
    short_output = output[split:].reshape(short_input.shape)
    short_grad = grad_input[split:].reshape(short_input.shape)
    return (
        long_output,
        short_output,
        long_grad,
        short_grad,
        updated[0],
        updated[1],
        updated[2],
        updated[3],
        new_momenta[0],
        new_momenta[1],
        new_momenta[2],
        new_momenta[3],
        new_errors[0],
        new_errors[1],
        new_errors[2],
        new_errors[3],
        new_factors[0],
        new_factors[1],
        new_factors[2],
        new_factors[3],
        updated_vectors,
        momenta_vectors,
    )


def solution(mesh):
    in_specs = (
        P("rep", None, "seq", None),
        P("rep", "seq", None),
        P("rep", None, "seq", None),
        P("rep", "seq", None),
        P("rep", None),
        P("seq", "rep"),
        P("seq", "rep"),
        P("seq", "rep"),
        P("seq", "rep"),
        P("seq", "rep"),
        P("seq", "rep"),
        P("seq", "rep"),
        P("seq", "rep"),
        P("rep", "seq", None),
        P("rep", "seq", None),
        P("rep", "seq", None),
        P("rep", "seq", None),
        P(),
        P(),
        P(),
        P(),
        P(),
        P(),
    )
    out_specs = (
        P("rep", None, "seq", None),
        P("rep", "seq", None),
        P("rep", None, "seq", None),
        P("rep", "seq", None),
        P("seq", "rep"),
        P("seq", "rep"),
        P("seq", "rep"),
        P("seq", "rep"),
        P("seq", "rep"),
        P("seq", "rep"),
        P("seq", "rep"),
        P("seq", "rep"),
        P("rep", "seq", None),
        P("rep", "seq", None),
        P("rep", "seq", None),
        P("rep", "seq", None),
        P(),
        P(),
        P(),
        P(),
        P(),
        P(),
    )
    return jax.shard_map(local, mesh=mesh, in_specs=in_specs, out_specs=out_specs, check_vma=False)
```

time: 1010 us -> 627 us (0.62)
  matrix products: 313 us -> 82 us
  waiting for transfers between devices: 433 us -> 214 us
  local copies, waits for them, and re-layouts: 66.9 us -> 138 us
  blocking collectives: 102 us -> 47.4 us
  Pallas kernels: 3.23 us -> 44 us
  starting transfers between devices: 1.97 us -> 42 us
  other arithmetic: 62.4 us -> 35.9 us
    dot_general x12 -> x0, matrix products: 193 us -> none  [the longest x2 65.8 us: run_layer(): jnp.einsum('bhqk,bkhd->bqhd', grad_scores, key_heads, preferred_element_t...]
    ppermute x0 -> x27, waiting for transfers between devices: none -> 148 us  [swap_with(): lax.ppermute(values, axis, [(source, source ^ distance) for source in ran...]
    reduce_scatter x8 -> x0, waiting for transfers between devices: 138 us -> none  [the longest x1 55.1 us: local(): lax.psum_scatter(local_grads[2].astype(jnp.bfloat16), 'seq', scatter_dime...]
    psum x1 -> x0, waiting for transfers between devices: 120 us -> none  [local(): lax.psum(jnp.concatenate(partial_q + [vector_total.reshape(rank, -1)], ax...]
    all_gather x8 -> x3, waiting for transfers between devices: 174 us -> 66.2 us  [gather_weights(): lax.all_gather(pack, ('seq', 'rep'), axis=0, tiled=False)]
    all_gather x5 -> x0, blocking collectives: 71.8 us -> none  [the longest x1 24.7 us: local(): lax.all_gather(master_attend.astype(jnp.bfloat16), 'rep', axis=1, tiled=T...]
    all_to_all x0 -> x1, blocking collectives: none -> 47.4 us  [exchange(): lax.all_to_all(values, 'seq', split_axis=0, concat_axis=0, tiled=True)]
    pallas_call x1 -> x3, Pallas kernels: 3.23 us -> 44 us  [the longest x1 23.5 us: run_layer(): backward_call(docs, by_heads, grad_heads, long_log, short_log)]
  transfers between devices with their start and end apart: 17 -> 33, of which waited for: 10 -> 19; matrix products, arithmetic and copies ran while one was open for 38% -> 25% of each run, Pallas kernels for 0% -> 7%
where the time goes in v2:
time: 627 us; the launch traced here: 618 us
  waiting for transfers between devices  214 us (34%)
  local copies, waits for them, and re-layouts  138 us (22%)
  matrix products  82 us (13%)
  blocking collectives  47.4 us (8%)
  Pallas kernels  44 us (7%)
  starting transfers between devices  42 us (7%)
  other arithmetic  35.9 us (6%)
  between operations  15.6 us (2%)
    ppermute x27, waiting for transfers between devices, swap_with(): lax.ppermute(values, axis, [(source, source ^ distance) for source in ran...  148 us
    all_gather x3, waiting for transfers between devices, gather_weights(): lax.all_gather(pack, ('seq', 'rep'), axis=0, tiled=False)  66.2 us
    all_to_all x1, blocking collectives, exchange(): lax.all_to_all(values, 'seq', split_axis=0, concat_axis=0, tiled=True)  47.4 us
    unnamed x176, local copies, waits for them, and re-layouts  37.3 us
    ppermute x27, starting transfers between devices, swap_with(): lax.ppermute(values, axis, [(source, source ^ distance) for source in ran...  27.8 us
    dot_general x8, matrix products, contract_rows(): lax.dot_general(left, right, (((0,), (0,)), ((), ())), precision=precisio...  26.9 us
    pallas_call x1, Pallas kernels, run_layer(): backward_call(docs, by_heads, grad_heads, long_log, short_log)  23.5 us
    another operation x2, local copies, waits for them, and re-layouts, gather_weights(): whole[2].reshape(seq_count, rep_count, rows, pieces, contract.shape[1])  21.9 us
  transfers between devices with their start and end apart: 33, of which 19 were waited for; matrix products, arithmetic and copies ran while one was open for 25% of the time, Pallas kernels for 7%

profile of v2, /device:TPU:0, one launch (start us, length us, event | category | flops | bytes accessed | tf_op | source)
XLA Modules:
  0.0 618.3 jit_solution(17474083932802582468)
XLA Ops:
  14.1 63.9 %all-gather.7.cloned.1.call-done = bf16[6144,384]{1,0:T(8,128)(2,1)} async-done(((bf16[192,384]{1,0:T(8,128)(2,1)}), bf16[6144,384]{1,0:T(8,128)(2,1)}) %all-gather.7.cloned.1.call-update) | async-done | bytes 4718608 | tf_op jit(solution)/shard_map/all_gather | solution.py:427
  78.0 7.3 %copy.97 = bf16[4,8,192,288]{3,1,2,0:T(8,128)(2,1)} copy(bf16[4,8,192,288]{3,2,1,0:T(8,128)(2,1)} %bitcast.211) | data formatting | bytes 7077888
  85.3 8.0 %reshape.229 = bf16[768,2304]{1,0:T(8,128)(2,1)} reshape(bf16[4,192,8,288]{3,2,1,0:T(8,128)(2,1)} %bitcast.200) | data formatting | bytes 7077888 | tf_op jit(solution)/shard_map/reshape | solution.py:434
  93.4 6.3 %add_convert_fusion = bf16[640,2304]{1,0:T(8,128)(2,1)} fusion(bf16[768,2304]{1,0:T(8,128)(2,1)} %reshape.229, f32[2304]{0:T(1024)S(1)} %pad_maximum_fusion.5, f32[768]{0:T(1024)S(1)} %get-tuple-element.145, f32[768]{0:T(1024)S(1)} %get-tuple-element.146, f32[640]{0:T(1024)S(1)} %fusion.50, f32[640]{0:T(1024)S(1)} %broadcast_multiply_fusion.1, ...), kind=kOutput, calls=%fused_computation.10 | convolution fusion | flops 2272296960 | bytes 7491584 | tf_op jit(solution)/shard_map/dot_general | solution.py:344
  99.6 5.5 copy.67
  107.2 47.4 %all_to_all.20 = bf16[4,640,576]{1,2,0:T(8,128)(2,1)} all-to-all(bf16[4,640,576]{1,2,0:T(8,128)(2,1)S(1)} %bitcast.210), channel_id=1, replica_groups=mesh['seq'=4,'rep'=8] {'seq'}, dimensions={0} | all-to-all | bytes 5898240 | tf_op jit(solution)/shard_map/all_to_all | solution.py:135
  154.6 4.7 copy.69.joined_ref
  159.3 17.3 %attention_forward.1 = (bf16[4,640,192]{2,1,0:T(8,128)(2,1)}, f32[2,4,3,256]{3,2,1,0:T(4,128)}, f32[4,3,128]{2,1,0:T(4,128)}) custom-call(s32[1,4]{1,0:T(1,128)} %docs_ref.3, bf16[4,640,576]{2,1,0:T(8,128)(2,1)} %copy.69.joined_ref), custom_call_target="tpu_custom_call" | custom-call | tf_op jit(solution)/shard_map/attention_forward/pallas_call | solution.py:352
  179.0 4.5 all-to-all-start.1
  189.8 3.8 reshape.233
  193.6 12.4 %reshape_reshape.3 = bf16[4,8,192,4,96]{4,3,2,1,0:T(4,128)(2,1)} reshape(bf16[6144,384]{1,0:T(8,128)(2,1)} %all-gather.11.cloned.1.call-done) | data formatting | bytes 9437184 | tf_op jit(solution)/shard_map/reshape;reshape | solution.py:437
  205.9 9.5 %copy.96 = bf16[4,8,192,4,96]{4,1,2,3,0:T(8,128)(2,1)} copy(bf16[4,8,192,4,96]{4,3,2,1,0:T(4,128)(2,1)} %reshape_reshape.3) | data formatting | bytes 9437184 | tf_op jit(solution)/shard_map/reshape;reshape | solution.py:437
  215.5 11.3 %reshape.236 = bf16[3072,768]{1,0:T(8,128)(2,1)} reshape(bf16[4,4,192,8,96]{4,3,2,1,0:T(8,128)(2,1)} %bitcast.198) | data formatting | bytes 9437184 | tf_op jit(solution)/shard_map/reshape | solution.py:442
  229.1 5.2 copy.72
  244.3 9.9 %fusion.68 = (f32[3072]{0:T(1024)}, bf16[640,3072]{1,0:T(8,128)(2,1)S(1)}) fusion(f32[640,3072]{1,0:T(8,128)S(1)} %fusion.57, f32[3072]{0:T(1024)S(1)} %slice.140, bf16[3072,768]{1,0:T(8,128)(2,1)S(1)} %bitcast.224, bf16[128,768]{1,0:T(8,128)(2,1)S(1)} %bitcast.248, bf16[512,768]{1,0:T(8,128)(2,1)S(1)} %bitcast.242), kind=kOutput, calls=%fused_computation.191 | convolution fusion | flops 3065115648 | bytes 17522688 | tf_op jit(solution)/shard_map/dot_general | solution.py:86
  254.2 4.2 multiply_reduce_fusion
  258.4 6.3 %convolution_convert_fusion.1 = bf16[768,3072]{1,0:T(8,128)(2,1)} fusion(bf16[640,3072]{1,0:T(8,128)(2,1)S(1)} %get-tuple-element.153, f32[640,768]{1,0:T(8,128)S(1)} %get-tuple-element.149, f32[768]{0:T(1024)S(1)} %get-tuple-element.141, f32[768]{0:T(1024)S(1)} %get-tuple-element.140, f32[640]{0:T(1024)S(1)} %fusion.51, f32[640]{0:T(1024)S(1)} %broadcast_multiply_fusion), kind=kOutput, calls=%fused_computation.12 | convolution fusion | flops 3024715776 | bytes 10628096 | tf_op jit(solution)/shard_map/dot_general | solution.py:76
  271.4 7.0 %convolution_convert_fusion = bf16[3072,768]{1,0:T(8,128)(2,1)} fusion(bf16[128,768]{1,0:T(8,128)(2,1)S(1)} %bitcast.251, bf16[512,768]{1,0:T(8,128)(2,1)S(1)} %bitcast.245, f32[640,3072]{1,0:T(8,128)S(1)} %fusion.57, f32[3072]{0:T(1024)S(1)} %slice.140), kind=kOutput, calls=%fused_computation.11 | convolution fusion | flops 3043885056 | bytes 13578240 | tf_op jit(solution)/shard_map/dot_general | solution.py:76
  280.6 4.6 all-to-all-start.2
  314.6 16.6 %collective-permute-done.6 = bf16[2,192,384]{2,1,0:T(8,128)(2,1)} collective-permute-done((bf16[2,192,384]{2,1,0:T(8,128)(2,1)}, bf16[2,192,384]{2,1,0:T(8,128)(2,1)}, u32[]{:S(2)}, u32[]{:S(2)}) %collective-permute-start.6) | collective-permute-done | bytes 294944 | tf_op jit(solution)/shard_map/ppermute | solution.py:97
  335.6 25.5 %collective-permute-done.7 = bf16[192,384]{1,0:T(8,128)(2,1)S(1)} collective-permute-done((bf16[192,384]{1,0:T(8,128)(2,1)S(1)}, bf16[192,384]{1,0:T(8,128)(2,1)S(1)}, u32[]{:S(2)}, u32[]{:S(2)}) %collective-permute-start.7) | collective-permute-done | bytes 147488 | tf_op jit(solution)/shard_map/ppermute | solution.py:97
  361.9 4.4 collective-permute-done.5
  370.0 23.5 %attention_backward.1 = (bf16[4,640,576]{2,1,0:T(8,128)(2,1)}, f32[2,192]{1,0:T(2,128)}) custom-call(s32[1,4]{1,0:T(1,128)} %docs_ref.3, bf16[4,640,576]{2,1,0:T(8,128)(2,1)} %copy.69.joined_ref, bf16[4,640,192]{2,1,0:T(8,128)(2,1)} %copy.77.grad_ref, f32[2,4,3,256]{3,2,1,0:T(4,128)} %get-tuple-element.28.long_log_ref, ...), custom_call_target="tpu_custom_call" | custom-call | tf_op jit(solution)/shard_map/attention_backward/pallas_call | solution.py:376
  393.5 4.7 copy.78
  398.2 4.9 all-to-all-start.3
  415.0 44.6 %collective-permute-done.15 = bf16[768,384]{0,1:T(8,128)(2,1)S(1)} collective-permute-done((bf16[768,384]{0,1:T(8,128)(2,1)S(1)}, bf16[768,384]{0,1:T(8,128)(2,1)S(1)}, u32[]{:S(2)}, u32[]{:S(2)}) %collective-permute-start.15) | collective-permute-done | bytes 589856 | tf_op jit(solution)/shard_map/ppermute | solution.py:97
  483.6 12.1 %collective-permute-done.2 = bf16[2,192,1152]{2,1,0:T(8,128)(2,1)S(1)} collective-permute-done((bf16[2,192,1152]{2,1,0:T(8,128)(2,1)S(1)}, bf16[2,192,1152]{2,1,0:T(8,128)(2,1)S(1)}, u32[]{:S(2)}, u32[]{:S(2)}) %collective-permute-start.2) | collective-permute-done | bytes 884768 | tf_op jit(solution)/shard_map/ppermute | solution.py:97
  500.4 5.6 collective-permute-done.3
  541.6 4.3 collective-permute-done.22
  546.7 5.7 collective-permute-done.23
  557.5 10.4 %add_add_fusion.3 = f32[640,768]{1,0:T(8,128)S(1)} fusion(f32[640,768]{1,0:T(8,128)} %copy-done.26, bf16[3072,768]{1,0:T(8,128)(2,1)} %reshape.236, f32[768]{0:T(1024)S(1)} %copy-done.69, f32[640,3072]{1,0:T(8,128)} %copy-done.72, f32[3072]{0:T(1024)S(1)} %copy-done.67), kind=kOutput, calls=%fused_computation.54 | convolution fusion | flops 3040542720 | bytes 16530432 | tf_op jit(solution)/shard_map/dot_general | solution.py:361
  573.1 12.7 %collective-permute-done.26 = f32[8,8064]{1,0:T(8,128)S(1)} collective-permute-done((f32[8,8064]{1,0:T(8,128)S(1)}, f32[8,8064]{1,0:T(8,128)S(1)}, u32[]{:S(2)}, u32[]{:S(2)}) %collective-permute-start.26) | collective-permute-done | bytes 258080 | tf_op jit(solution)/shard_map/ppermute | solution.py:97
  (354 shorter events, 188.7 us)
Async XLA Ops:
  7.2 70.8 %all-gather.7.cloned.1.call-start = ((), (), s32[]{:S(2)}) async-start(), calls=%async_computation.4 | async-start | bytes 4866048 | tf_op jit(solution)/shard_map/all_gather | solution.py:427
  10.0 183.5 %all-gather.11.cloned.1.call-start = ((), (), s32[]{:S(2)}) async-start(), calls=%async_computation.6 | async-start | bytes 4866048 | tf_op jit(solution)/shard_map/all_gather | solution.py:427
  12.1 217.0 %all-gather.9.cloned.1.call-start = ((), (), s32[]{:S(2)}) async-start(), calls=%async_computation.5 | async-start | bytes 4866048 | tf_op jit(solution)/shard_map/all_gather | solution.py:427
  179.0 58.6 %all-to-all-start.1 = ((bf16[4,640,192]{1,2,0:T(8,128)(2,1)}), bf16[4,640,192]{1,2,0:T(8,128)(2,1)}, u32[]{:S(2)}, u32[]{:S(2)}) async-start(bf16[4,640,192]{1,2,0:T(8,128)(2,1)} %copy.70), calls=%async_computation.1 | async-start | bytes 1966080 | tf_op jit(solution)/shard_map/all_to_all | solution.py:135
  280.6 87.0 %all-to-all-start.2 = ((bf16[4,640,192]{1,2,0:T(8,128)(2,1)}), bf16[4,640,192]{1,2,0:T(8,128)(2,1)}, u32[]{:S(2)}, u32[]{:S(2)}) async-start(bf16[4,640,192]{1,2,0:T(8,128)(2,1)} %bitcast.225), calls=%async_computation.2 | async-start | bytes 1966080 | tf_op jit(solution)/shard_map/all_to_all | solution.py:135
  289.4 113.9 %collective-permute-start.10 = (bf16[2,192,1536]{2,1,0:T(8,128)(2,1)}, bf16[2,192,1536]{2,1,0:T(8,128)(2,1)}, u32[]{:S(2)}, u32[]{:S(2)}) collective-permute-start(bf16[2,192,1536]{2,1,0:T(8,128)(2,1)} %dynamic-slice_bitcast_fusion), channel_id=1, source_target_pairs={{0,16},{8,24},{16,0},{24,8},{1,17},{9,25},{17,1},{25,9},{2,18},{10... | collective-permute-start | bytes 3538952 | tf_op jit(solution)/shard_map/ppermute | solution.py:97
  292.5 120.6 %collective-permute-start.8 = (bf16[2,192,1536]{2,1,0:T(8,128)(2,1)}, bf16[2,192,1536]{2,1,0:T(8,128)(2,1)}, u32[]{:S(2)}, u32[]{:S(2)}) collective-permute-start(bf16[2,192,1536]{2,1,0:T(8,128)(2,1)} %dynamic-slice_bitcast_fusion.1), channel_id=1, source_target_pairs={{0,8},{8,0},{16,24},{24,16},{1,9},{9,1},{17,25},{25,17},{2,10},{10... | collective-permute-start | bytes 3538952 | tf_op jit(solution)/shard_map/ppermute | solution.py:97
  295.0 36.2 %collective-permute-start.6 = (bf16[2,192,384]{2,1,0:T(8,128)(2,1)}, bf16[2,192,384]{2,1,0:T(8,128)(2,1)}, u32[]{:S(2)}, u32[]{:S(2)}) collective-permute-start(bf16[2,192,384]{2,1,0:T(8,128)(2,1)} %dynamic-slice_bitcast_fusion.10), channel_id=1, source_target_pairs={{0,16},{8,24},{16,0},{24,8},{1,17},{9,25},{17,1},{25,9},{2,18},{10... | collective-permute-start | bytes 884744 | tf_op jit(solution)/shard_map/ppermute | solution.py:97
  296.4 37.4 %collective-permute-start.4 = (bf16[2,192,384]{2,1,0:T(8,128)(2,1)}, bf16[2,192,384]{2,1,0:T(8,128)(2,1)}, u32[]{:S(2)}, u32[]{:S(2)}) collective-permute-start(bf16[2,192,384]{2,1,0:T(8,128)(2,1)} %dynamic-slice_bitcast_fusion.11), channel_id=1, source_target_pairs={{0,8},{8,0},{16,24},{24,16},{1,9},{9,1},{17,25},{25,17},{2,10},{10... | collective-permute-start | bytes 884744 | tf_op jit(solution)/shard_map/ppermute | solution.py:97
  302.8 104.7 %collective-permute-start.14 = (bf16[2,768,384]{1,2,0:T(8,128)(2,1)}, bf16[2,768,384]{1,2,0:T(8,128)(2,1)}, u32[]{:S(2)}, u32[]{:S(2)}) collective-permute-start(bf16[2,768,384]{1,2,0:T(8,128)(2,1)} %bitcast.239), channel_id=1, source_target_pairs={{0,16},{8,24},{16,0},{24,8},{1,17},{9,25},{17,1},{25,9},{2,18},{10... | collective-permute-start | bytes 3538952 | tf_op jit(solution)/shard_map/ppermute | solution.py:97
  331.2 78.2 %collective-permute-start.12 = (bf16[2,768,384]{1,2,0:T(8,128)(2,1)}, bf16[2,768,384]{1,2,0:T(8,128)(2,1)}, u32[]{:S(2)}, u32[]{:S(2)}) collective-permute-start(bf16[2,768,384]{1,2,0:T(8,128)(2,1)} %bitcast.240), channel_id=1, source_target_pairs={{0,8},{8,0},{16,24},{24,16},{1,9},{9,1},{17,25},{25,17},{2,10},{10... | collective-permute-start | bytes 3538952 | tf_op jit(solution)/shard_map/ppermute | solution.py:97
  333.8 27.3 %collective-permute-start.7 = (bf16[192,384]{1,0:T(8,128)(2,1)S(1)}, bf16[192,384]{1,0:T(8,128)(2,1)S(1)}, u32[]{:S(2)}, u32[]{:S(2)}) collective-permute-start(bf16[192,384]{1,0:T(8,128)(2,1)S(1)} %dynamic-slice_bitcast_fusion.12), channel_id=1, source_target_pairs={{0,8},{8,0},{16,24},{24,16},{1,9},{9,1},{17,25},{25,17},{2,10},{10... | collective-permute-start | bytes 442376 | tf_op jit(solution)/shard_map/ppermute | solution.py:97
  361.1 5.1 collective-permute-start.5
  398.2 69.1 %all-to-all-start.3 = ((bf16[4,640,576]{1,2,0:T(8,128)(2,1)}), bf16[4,640,576]{1,2,0:T(8,128)(2,1)}, u32[]{:S(2)}, u32[]{:S(2)}) async-start(bf16[4,640,576]{1,2,0:T(8,128)(2,1)} %copy.78), calls=%async_computation.3 | async-start | bytes 5898240 | tf_op jit(solution)/shard_map/all_to_all | solution.py:135
  405.4 57.7 %collective-permute-start.11 = (bf16[192,1536]{1,0:T(8,128)(2,1)S(1)}, bf16[192,1536]{1,0:T(8,128)(2,1)S(1)}, u32[]{:S(2)}, u32[]{:S(2)}) collective-permute-start(bf16[192,1536]{1,0:T(8,128)(2,1)S(1)} %dynamic-slice_bitcast_fusion.6), channel_id=1, source_target_pairs={{0,8},{8,0},{16,24},{24,16},{1,9},{9,1},{17,25},{25,17},{2,10},{10... | collective-permute-start | bytes 1769480 | tf_op jit(solution)/shard_map/ppermute | solution.py:97
  409.2 50.3 %collective-permute-start.15 = (bf16[768,384]{0,1:T(8,128)(2,1)S(1)}, bf16[768,384]{0,1:T(8,128)(2,1)S(1)}, u32[]{:S(2)}, u32[]{:S(2)}) collective-permute-start(bf16[768,384]{0,1:T(8,128)(2,1)S(1)} %dynamic-slice_bitcast_fusion.4), channel_id=1, source_target_pairs={{0,8},{8,0},{16,24},{24,16},{1,9},{9,1},{17,25},{25,17},{2,10},{10... | collective-permute-start | bytes 1769480 | tf_op jit(solution)/shard_map/ppermute | solution.py:97
  411.2 48.5 %collective-permute-start.13 = (bf16[768,384]{0,1:T(8,128)(2,1)S(1)}, bf16[768,384]{0,1:T(8,128)(2,1)S(1)}, u32[]{:S(2)}, u32[]{:S(2)}) collective-permute-start(bf16[768,384]{0,1:T(8,128)(2,1)S(1)} %dynamic-slice_bitcast_fusion.5), channel_id=1, source_target_pairs={{0,16},{8,24},{16,0},{24,8},{1,17},{9,25},{17,1},{25,9},{2,18},{10... | collective-permute-start | bytes 1769480 | tf_op jit(solution)/shard_map/ppermute | solution.py:97
  414.7 48.6 %collective-permute-start.9 = (bf16[192,1536]{1,0:T(8,128)(2,1)S(1)}, bf16[192,1536]{1,0:T(8,128)(2,1)S(1)}, u32[]{:S(2)}, u32[]{:S(2)}) collective-permute-start(bf16[192,1536]{1,0:T(8,128)(2,1)S(1)} %dynamic-slice_bitcast_fusion.7), channel_id=1, source_target_pairs={{0,16},{8,24},{16,0},{24,8},{1,17},{9,25},{17,1},{25,9},{2,18},{10... | collective-permute-start | bytes 1769480 | tf_op jit(solution)/shard_map/ppermute | solution.py:97
  477.4 18.2 %collective-permute-start.2 = (bf16[2,192,1152]{2,1,0:T(8,128)(2,1)S(1)}, bf16[2,192,1152]{2,1,0:T(8,128)(2,1)S(1)}, u32[]{:S(2)}, u32[]{:S(2)}) collective-permute-start(bf16[2,192,1152]{2,1,0:T(8,128)(2,1)S(1)} %dynamic-slice_bitcast_fusion.2), channel_id=1, source_target_pairs={{0,16},{8,24},{16,0},{24,8},{1,17},{9,25},{17,1},{25,9},{2,18},{10... | collective-permute-start | bytes 2654216 | tf_op jit(solution)/shard_map/ppermute | solution.py:97
  479.1 20.9 %collective-permute-start = (bf16[2,192,1152]{2,1,0:T(8,128)(2,1)S(1)}, bf16[2,192,1152]{2,1,0:T(8,128)(2,1)S(1)}, u32[]{:S(2)}, u32[]{:S(2)}) collective-permute-start(bf16[2,192,1152]{2,1,0:T(8,128)(2,1)S(1)} %dynamic-slice_bitcast_fusion.3), channel_id=1, source_target_pairs={{0,8},{8,0},{16,24},{24,16},{1,9},{9,1},{17,25},{25,17},{2,10},{10... | collective-permute-start | bytes 2654216 | tf_op jit(solution)/shard_map/ppermute | solution.py:97
  495.9 10.1 %collective-permute-start.3 = (bf16[192,1152]{1,0:T(8,128)(2,1)S(1)}, bf16[192,1152]{1,0:T(8,128)(2,1)S(1)}, u32[]{:S(2)}, u32[]{:S(2)}) collective-permute-start(bf16[192,1152]{1,0:T(8,128)(2,1)S(1)} %dynamic-slice_bitcast_fusion.8), channel_id=1, source_target_pairs={{0,8},{8,0},{16,24},{24,16},{1,9},{9,1},{17,25},{25,17},{2,10},{10... | collective-permute-start | bytes 1327112 | tf_op jit(solution)/shard_map/ppermute | solution.py:97
  500.3 8.4 %collective-permute-start.1 = (bf16[192,1152]{1,0:T(8,128)(2,1)S(1)}, bf16[192,1152]{1,0:T(8,128)(2,1)S(1)}, u32[]{:S(2)}, u32[]{:S(2)}) collective-permute-start(bf16[192,1152]{1,0:T(8,128)(2,1)S(1)} %dynamic-slice_bitcast_fusion.9), channel_id=1, source_target_pairs={{0,16},{8,24},{16,0},{24,8},{1,17},{9,25},{17,1},{25,9},{2,18},{10... | collective-permute-start | bytes 1327112 | tf_op jit(solution)/shard_map/ppermute | solution.py:97
  511.7 4.2 collective-permute-start.17
  515.8 5.1 collective-permute-start.18
  520.9 5.1 collective-permute-start.21
  521.0 5.0 collective-permute-start.20
  522.3 4.3 collective-permute-start.19
  539.5 6.4 %collective-permute-start.22 = (f32[8,8064]{1,0:T(8,128)S(1)}, f32[8,8064]{1,0:T(8,128)S(1)}, u32[]{:S(2)}, u32[]{:S(2)}) collective-permute-start(f32[8,8064]{1,0:T(8,128)S(1)} %constant_dynamic-update-slice_fusion.1), channel_id=1, source_target_pairs={{0,8},{8,0},{16,24},{24,16},{1,9},{9,1},{17,25},{25,17},{2,10},{10... | collective-permute-start | bytes 774152 | tf_op jit(solution)/shard_map/ppermute | solution.py:97
  546.0 6.4 %collective-permute-start.23 = (f32[8,8064]{1,0:T(8,128)S(1)}, f32[8,8064]{1,0:T(8,128)S(1)}, u32[]{:S(2)}, u32[]{:S(2)}) collective-permute-start(f32[8,8064]{1,0:T(8,128)S(1)} %add.332), channel_id=1, source_target_pairs={{0,16},{8,24},{16,0},{24,8},{1,17},{9,25},{17,1},{25,9},{2,18},{10... | collective-permute-start | bytes 774152 | tf_op jit(solution)/shard_map/ppermute | solution.py:97
  553.1 1.9 collective-permute-start.24
  556.1 15.2 %collective-permute-start.25 = (f32[8,8064]{1,0:T(8,128)S(1)}, f32[8,8064]{1,0:T(8,128)S(1)}, u32[]{:S(2)}, u32[]{:S(2)}) collective-permute-start(f32[8,8064]{1,0:T(8,128)S(1)} %add.334), channel_id=1, source_target_pairs={{0,2},{1,3},{2,0},{3,1},{4,6},{5,7},{6,4},{7,5},{8,10},{9,11},{10,... | collective-permute-start | bytes 774152 | tf_op jit(solution)/shard_map/ppermute | solution.py:97
  571.3 14.5 %collective-permute-start.26 = (f32[8,8064]{1,0:T(8,128)S(1)}, f32[8,8064]{1,0:T(8,128)S(1)}, u32[]{:S(2)}, u32[]{:S(2)}) collective-permute-start(f32[8,8064]{1,0:T(8,128)S(1)} %add.335), channel_id=1, source_target_pairs={{0,4},{1,5},{2,6},{3,7},{4,0},{5,1},{6,2},{7,3},{8,12},{9,13},{10,... | collective-permute-start | bytes 774152 | tf_op jit(solution)/shard_map/ppermute | solution.py:97
  (81 other events, 1080.8 us)
Sparse Core Ops, SparseCore 0:
  11.6 66.3 all-gather.6
  81.6 79.1 all-gather.10
  164.4 64.6 all-gather.8

commit v3 on v2

--- a/solution.py
+++ b/solution.py
@@ -97,11 +97,11 @@
     return lax.ppermute(values, axis, [(source, source ^ distance) for source in range(count)])
 
 
-def butterfly_sum(values, axis):
-    distance = 1
-    while distance < lax.axis_size(axis):
+def butterfly_sum(values, axis, first=1):
+    count = lax.axis_size(axis)
+    distances = [1 << bit for bit in range(count.bit_length() - 1)]
+    for distance in [d for d in distances if d >= first] + [d for d in distances if d < first]:
         values = values + swap_with(values, axis, distance)
-        distance *= 2
     return values
 
 
@@ -412,15 +412,22 @@
     return output, grad_input, operands, vector_grad
 
 
-def gather_weights(masters):
+def pack_weights(masters):
     attend, merge, expand, contract = (master.astype(jnp.bfloat16) for master in masters)
     rows = attend.shape[0]
     pieces = contract.shape[0] // rows
-    packs = (
+    return (
         jnp.concatenate([attend, merge], axis=1),
         expand,
         jnp.concatenate([contract[at * rows : (at + 1) * rows] for at in range(pieces)], axis=1),
     )
+
+
+def gather_plain(masters):
+    packs = pack_weights(masters)
+    rows = packs[0].shape[0]
+    split = masters[0].shape[1]
+    pieces = masters[3].shape[0] // rows
     seq_count = lax.axis_size("seq")
     rep_count = lax.axis_size("rep")
     whole = [
@@ -433,14 +440,100 @@
     def join(blocks):
         return blocks.transpose(0, 2, 1, 3).reshape(seq_count * rows, -1)
 
-    split = attend.shape[1]
-    contract_blocks = whole[2].reshape(seq_count, rep_count, rows, pieces, contract.shape[1])
+    contract_blocks = whole[2].reshape(seq_count, rep_count, rows, pieces, masters[3].shape[1])
     return (
         join(whole[0][..., :split]),
         join(whole[0][..., split:]),
         join(whole[1]),
         contract_blocks.transpose(0, 3, 2, 1, 4).reshape(seq_count * pieces * rows, -1),
     )
+
+
+def spread_pack(pack):
+    near = jnp.stack([pack, swap_with(pack, "rep", 2)])
+    far = jnp.stack([swap_with(pack, "rep", 4), swap_with(pack, "rep", 6)])
+    near = jnp.stack([near, swap_with(near, "seq", 1)])
+    far = jnp.stack([far, swap_with(far, "seq", 2)])
+    near = jnp.concatenate([near, swap_with(near, "seq", 2)])
+    far = jnp.concatenate([far, swap_with(far, "seq", 1)])
+    return near, far, swap_with(near, "rep", 1), swap_with(far, "rep", 1)
+
+
+def place_pack(spread, splits):
+    _, _, rows, lanes = spread[0].shape
+    here = jnp.stack([lax.axis_index("seq"), lax.axis_index("rep")]).astype(jnp.int32)
+    groups = []
+    low = 0
+    for split in splits:
+        widths = split if isinstance(split, tuple) else (split,)
+        group = []
+        for width in widths:
+            group.append((low, width))
+            low += width
+        groups.append(group)
+    count = 8
+
+    def kernel(here_ref, near_ref, far_ref, near_other_ref, far_other_ref, *outs):
+        rep = here_ref[1]
+        core = rep % 2
+        depth = rep // 2
+        columns = [None] * count
+        for at in range(count // 2):
+            low_bit = (at % 2 + depth) % 2
+            is_near = (at // 2 + depth // 2) % 2 == 0
+            own = jnp.where(is_near, near_ref[0, low_bit], far_ref[0, low_bit])
+            other = jnp.where(is_near, near_other_ref[0, low_bit], far_other_ref[0, low_bit])
+            columns[2 * at] = jnp.where(core == 0, own, other)
+            columns[2 * at + 1] = jnp.where(core == 0, other, own)
+        for out_ref, group in zip(outs, groups):
+            for number, (start, width) in enumerate(group):
+                out_ref[number * rows : (number + 1) * rows, :] = jnp.concatenate(
+                    [column[:, start : start + width] for column in columns], axis=1
+                )
+
+    def near_map(distance, here_ref):
+        return (distance, 0, 0, 0)
+
+    def far_map(distance, here_ref):
+        return ((distance % 2) * 2 + distance // 2, 0, 0, 0)
+
+    def out_map(distance, here_ref):
+        seq = here_ref[0]
+        return ((distance // 2 + seq // 2) % 2 * 2 + (distance + seq) % 2, 0)
+
+    block = (1, 2, rows, lanes)
+    shapes = [(len(group) * rows, count * group[0][1]) for group in groups]
+    return pl.pallas_call(
+        kernel,
+        grid_spec=pltpu.PrefetchScalarGridSpec(
+            num_scalar_prefetch=1,
+            grid=(4,),
+            in_specs=[
+                pl.BlockSpec(block, near_map),
+                pl.BlockSpec(block, far_map),
+                pl.BlockSpec(block, near_map),
+                pl.BlockSpec(block, far_map),
+            ],
+            out_specs=[pl.BlockSpec(shape, out_map) for shape in shapes],
+        ),
+        out_shape=[
+            jax.ShapeDtypeStruct((4 * shape[0], shape[1]), jnp.bfloat16) for shape in shapes
+        ],
+        name="place_weights",
+    )(here, *spread)
+
+
+def gather_weights(masters):
+    if lax.axis_size("seq") != 4 or lax.axis_size("rep") != 8:
+        return gather_plain(masters)
+    packs = pack_weights(masters)
+    pieces = masters[3].shape[0] // masters[0].shape[0]
+    attend, merge = place_pack(
+        spread_pack(packs[0]), (masters[0].shape[1], masters[1].shape[1])
+    )
+    (expand,) = place_pack(spread_pack(packs[1]), (masters[2].shape[1],))
+    (contract,) = place_pack(spread_pack(packs[2]), ((masters[3].shape[1],) * pieces,))
+    return attend, merge, expand, contract
 
 
 def local(
@@ -524,7 +617,14 @@
         )
     rank = projected.shape[0]
     renewed_all = jnp.concatenate(partial_q + [vector_total.reshape(rank, -1)], axis=1)
-    renewed_all = butterfly_sum(butterfly_sum(renewed_all, "seq"), "rep")
+    middle = renewed_all.shape[1] // 2 // LANES * LANES
+    renewed_all = jnp.concatenate(
+        [
+            butterfly_sum(butterfly_sum(renewed_all[:, :middle], "seq"), "rep"),
+            butterfly_sum(butterfly_sum(renewed_all[:, middle:], "rep", 2), "seq"),
+        ],
+        axis=1,
+    )
     renewed_all = renewed_all / rep_count
     updated = []
     new_momenta = []

time: 627 us -> 575 us (0.917)
  local copies, waits for them, and re-layouts: 138 us -> 73.9 us
  blocking collectives: 47.4 us -> 0 us
  starting transfers between devices: 42 us -> 77.8 us
  Pallas kernels: 44 us -> 62.7 us
  other arithmetic: 35.9 us -> 50 us
  between operations: 15.6 us -> 2.49 us
  waiting for transfers between devices: 214 us -> 221 us
    ppermute x27 -> x59, waiting for transfers between devices: 148 us -> 221 us  [swap_with(): lax.ppermute(values, axis, [(source, source ^ distance) for source in ran...]
    all_gather x3 -> x0, waiting for transfers between devices: 66.2 us -> none  [gather_weights(): lax.all_gather(pack, ('seq', 'rep'), axis=0, tiled=False)]
    all_to_all x1 -> x0, blocking collectives: 47.4 us -> none  [exchange(): lax.all_to_all(values, 'seq', split_axis=0, concat_axis=0, tiled=True)]
    ppermute x27 -> x59, starting transfers between devices: 27.8 us -> 58.6 us  [swap_with(): lax.ppermute(values, axis, [(source, source ^ distance) for source in ran...]
    reshape x4 -> x0, local copies, waits for them, and re-layouts: 28.2 us -> none  [the longest x2 11.8 us: join(): return blocks.transpose(0, 2, 1, 3).reshape(seq_count * rows, -1)]
    another operation x2 -> x0, local copies, waits for them, and re-layouts: 21.9 us -> none  [gather_weights(): whole[2].reshape(seq_count, rep_count, rows, pieces, contract.shape[1])]
    pallas_call x0 -> x3, Pallas kernels: none -> 18.8 us  [place_pack(): pl.pallas_call(kernel, grid_spec=pltpu.PrefetchScalarGridSpec(num_scalar_...]
    unnamed x176 -> x219, local copies, waits for them, and re-layouts: 37.3 us -> 22.7 us
  transfers between devices with their start and end apart: 33 -> 63, of which waited for: 19 -> 28; matrix products, arithmetic and copies ran while one was open for 25% -> 19% of each run, Pallas kernels for 7% -> 10%
where the time goes in v3:
time: 575 us; the launch traced here: 568 us
  waiting for transfers between devices  221 us (38%)
  matrix products  80.4 us (14%)
  starting transfers between devices  77.8 us (14%)
  local copies, waits for them, and re-layouts  73.9 us (13%)
  Pallas kernels  62.7 us (11%)
  other arithmetic  50 us (9%)
    ppermute x59, waiting for transfers between devices, swap_with(): lax.ppermute(values, axis, [(source, source ^ distance) for source in ran...  221 us
    ppermute x59, starting transfers between devices, swap_with(): lax.ppermute(values, axis, [(source, source ^ distance) for source in ran...  58.6 us
    dot_general x8, matrix products, contract_rows(): lax.dot_general(left, right, (((0,), (0,)), ((), ())), precision=precisio...  26.9 us
    pallas_call x1, Pallas kernels, run_layer(): backward_call(docs, by_heads, grad_heads, long_log, short_log)  23.5 us
    unnamed x219, local copies, waits for them, and re-layouts  22.7 us
    all_to_all x4, starting transfers between devices, exchange(): lax.all_to_all(values, 'seq', split_axis=0, concat_axis=0, tiled=True)  19.1 us
    dot_general x4, matrix products, contract_cols(): lax.dot_general(left, right, (((1,), (1,)), ((), ())), precision=precisio...  18.9 us
    pallas_call x3, Pallas kernels, place_pack(): pl.pallas_call(kernel, grid_spec=pltpu.PrefetchScalarGridSpec(num_scalar_...  18.8 us
  transfers between devices with their start and end apart: 63, of which 28 were waited for; matrix products, arithmetic and copies ran while one was open for 19% of the time, Pallas kernels for 10%

profile of v3, /device:TPU:0, one launch (start us, length us, event | category | flops | bytes accessed | tf_op | source)
XLA Modules:
  0.0 568.0 jit_solution(16343965016420296180)
XLA Ops:
  11.5 4.7 collective-permute-done.4
  16.2 5.2 collective-permute-done.3
  23.7 7.7 %collective-permute-done.5 = bf16[2,192,384]{2,1,0:T(8,128)(2,1)S(1)} collective-permute-done((bf16[2,192,384]{2,1,0:T(8,128)(2,1)S(1)}, bf16[2,192,384]{2,1,0:T(8,128)(2,1)S(1)}, u32[]{:S(2)}, u32[]{:S(2)}) %collective-permute-start.5) | collective-permute-done | bytes 294944 | tf_op jit(solution)/shard_map/ppermute | solution.py:97
  54.8 6.3 %place_weights.3 = (bf16[768,2304]{1,0:T(8,128)(2,1)}, bf16[768,768]{1,0:T(8,128)(2,1)}) custom-call(s32[2]{0:T(128)} %pad_add_fusion.here_ref, bf16[4,2,192,384]{3,2,1,0:T(8,128)(2,1)} %copy-done.36, bf16[4,2,192,384]{3,2,1,0:T(8,128)(2,1)} %copy-done.37, bf16[4,2,192,384]{3,2,1,0:T(8,128)(2,1)} %collective-permute-done.7.near_other_ref, ...), custom_call_target="tpu_custom_call" | custom-call | tf_op jit(solution)/shard_map/place_weights/pallas_call | solution.py:506
  61.1 6.2 %add_convert_fusion = bf16[640,2304]{1,0:T(8,128)(2,1)} fusion(bf16[768,2304]{1,0:T(8,128)(2,1)} %get-tuple-element.29, f32[2304]{0:T(1024)S(1)} %copy-done.85, f32[768]{0:T(1024)S(1)} %copy-done.87, f32[768]{0:T(1024)S(1)} %get-tuple-element.162, f32[640]{0:T(1024)S(1)} %fusion.54, f32[640]{0:T(1024)S(1)} %broadcast_multiply_fusion.1, ...), kind=kOutput, calls=%fused_computation.9 | convolution fusion | flops 2272296960 | bytes 7491584 | tf_op jit(solution)/shard_map/dot_general | solution.py:344
  67.3 5.4 copy.64
  76.4 4.9 all-to-all-start
  93.9 28.8 %collective-permute-done.23 = bf16[2,192,384]{2,1,0:T(8,128)(2,1)S(1)} collective-permute-done((bf16[2,192,384]{2,1,0:T(8,128)(2,1)S(1)}, bf16[2,192,384]{2,1,0:T(8,128)(2,1)S(1)}, u32[]{:S(2)}, u32[]{:S(2)}) %collective-permute-start.23) | collective-permute-done | bytes 294944 | tf_op jit(solution)/shard_map/ppermute | solution.py:97
  125.3 16.3 %collective-permute-done.14 = bf16[2,192,384]{2,1,0:T(8,128)(2,1)S(1)} collective-permute-done((bf16[2,192,384]{2,1,0:T(8,128)(2,1)S(1)}, bf16[2,192,384]{2,1,0:T(8,128)(2,1)S(1)}, u32[]{:S(2)}, u32[]{:S(2)}) %collective-permute-start.14) | collective-permute-done | bytes 294944 | tf_op jit(solution)/shard_map/ppermute | solution.py:97
  146.4 6.9 %collective-permute-done.11 = bf16[2,2,192,384]{3,2,1,0:T(8,128)(2,1)S(1)} collective-permute-done((bf16[2,2,192,384]{3,2,1,0:T(8,128)(2,1)S(1)}, bf16[2,2,192,384]{3,2,1,0:T(8,128)(2,1)S(1)}, u32[]{:S(2)}, u32[]{:S(2)}) %collective-permute-start.11) | collective-permute-done | bytes 589856 | tf_op jit(solution)/shard_map/ppermute | solution.py:97
  156.4 4.7 copy.66.joined_ref
  161.1 17.3 %attention_forward.1 = (bf16[4,640,192]{2,1,0:T(8,128)(2,1)}, f32[2,4,3,256]{3,2,1,0:T(4,128)}, f32[4,3,128]{2,1,0:T(4,128)}) custom-call(s32[1,4]{1,0:T(1,128)} %docs_ref.3, bf16[4,640,576]{2,1,0:T(8,128)(2,1)} %copy.66.joined_ref), custom_call_target="tpu_custom_call" | custom-call | tf_op jit(solution)/shard_map/attention_forward/pallas_call | solution.py:352
  180.7 4.7 all-to-all-start.1
  188.2 6.8 %place_weights.5 = bf16[3072,768]{1,0:T(8,128)(2,1)} custom-call(s32[2]{0:T(128)} %pad_add_fusion.here_ref, bf16[4,2,192,384]{3,2,1,0:T(8,128)(2,1)} %pad_maximum_fusion.4.near_ref, bf16[4,2,192,384]{3,2,1,0:T(8,128)(2,1)} %pad_maximum_fusion.5.far_ref, bf16[4,2,192,384]{3,2,1,0:T(8,128)(2,1)} %collective-permute-done.25.near_other_ref, ...), custom_call_target="tpu_custom_call" | custom-call | tf_op jit(solution)/shard_map/place_weights/pallas_call | solution.py:506
  195.0 5.8 %place_weights.4 = bf16[768,3072]{1,0:T(8,128)(2,1)} custom-call(s32[2]{0:T(128)} %pad_add_fusion.here_ref, bf16[4,2,192,384]{3,2,1,0:T(8,128)(2,1)} %pad_maximum_fusion.2.near_ref, bf16[4,2,192,384]{3,2,1,0:T(8,128)(2,1)} %pad_maximum_fusion.3.far_ref, bf16[4,2,192,384]{3,2,1,0:T(8,128)(2,1)} %collective-permute-done.16.near_other_ref, ...), custom_call_target="tpu_custom_call" | custom-call | tf_op jit(solution)/shard_map/place_weights/pallas_call | solution.py:506
  207.8 9.9 %fusion.78 = (f32[3072]{0:T(1024)}, bf16[640,3072]{1,0:T(8,128)(2,1)S(1)}) fusion(f32[640,3072]{1,0:T(8,128)S(1)} %fusion.67, f32[3072]{0:T(1024)S(1)} %slice.140, bf16[3072,768]{1,0:T(8,128)(2,1)S(1)} %bitcast.222, bf16[128,768]{1,0:T(8,128)(2,1)S(1)} %bitcast.264, bf16[512,768]{1,0:T(8,128)(2,1)S(1)} %bitcast.258), kind=kOutput, calls=%fused_computation.216 | convolution fusion | flops 3065115648 | bytes 17522688 | tf_op jit(solution)/shard_map/dot_general | solution.py:86
  221.9 6.2 %convolution_convert_fusion.1 = bf16[768,3072]{1,0:T(8,128)(2,1)} fusion(bf16[640,3072]{1,0:T(8,128)(2,1)S(1)} %get-tuple-element.169, f32[640,768]{1,0:T(8,128)S(1)} %get-tuple-element.165, f32[768]{0:T(1024)S(1)} %copy-done.88, f32[768]{0:T(1024)S(1)} %copy-done.80, f32[640]{0:T(1024)S(1)} %fusion.55, f32[640]{0:T(1024)S(1)} %broadcast_multiply_fusion), kind=kOutput, calls=%fused_computation.11 | convolution fusion | flops 3024715776 | bytes 10628096 | tf_op jit(solution)/shard_map/dot_general | solution.py:76
  234.8 7.0 %convolution_convert_fusion = bf16[3072,768]{1,0:T(8,128)(2,1)} fusion(bf16[128,768]{1,0:T(8,128)(2,1)S(1)} %bitcast.267, bf16[512,768]{1,0:T(8,128)(2,1)S(1)} %bitcast.261, f32[640,3072]{1,0:T(8,128)S(1)} %fusion.67, f32[3072]{0:T(1024)S(1)} %slice.140), kind=kOutput, calls=%fused_computation.10 | convolution fusion | flops 3043885056 | bytes 13578240 | tf_op jit(solution)/shard_map/dot_general | solution.py:76
  244.1 4.4 all-to-all-start.2
  277.9 16.6 %collective-permute-done.33 = bf16[2,192,384]{2,1,0:T(8,128)(2,1)} collective-permute-done((bf16[2,192,384]{2,1,0:T(8,128)(2,1)}, bf16[2,192,384]{2,1,0:T(8,128)(2,1)}, u32[]{:S(2)}, u32[]{:S(2)}) %collective-permute-start.33) | collective-permute-done | bytes 294944 | tf_op jit(solution)/shard_map/ppermute | solution.py:97
  299.0 26.0 %collective-permute-done.34 = bf16[192,384]{1,0:T(8,128)(2,1)S(1)} collective-permute-done((bf16[192,384]{1,0:T(8,128)(2,1)S(1)}, bf16[192,384]{1,0:T(8,128)(2,1)S(1)}, u32[]{:S(2)}, u32[]{:S(2)}) %collective-permute-start.34) | collective-permute-done | bytes 147488 | tf_op jit(solution)/shard_map/ppermute | solution.py:97
  325.6 4.5 collective-permute-done.32
  333.9 23.5 %attention_backward.1 = (bf16[4,640,576]{2,1,0:T(8,128)(2,1)}, f32[2,192]{1,0:T(2,128)}) custom-call(s32[1,4]{1,0:T(1,128)} %docs_ref.3, bf16[4,640,576]{2,1,0:T(8,128)(2,1)} %copy.66.joined_ref, bf16[4,640,192]{2,1,0:T(8,128)(2,1)} %copy.71.grad_ref, f32[2,4,3,256]{3,2,1,0:T(4,128)} %get-tuple-element.32.long_log_ref, ...), custom_call_target="tpu_custom_call" | custom-call | tf_op jit(solution)/shard_map/attention_backward/pallas_call | solution.py:376
  357.4 4.7 copy.72
  362.0 5.2 all-to-all-start.3
  379.6 44.5 %collective-permute-done.42 = bf16[768,384]{0,1:T(8,128)(2,1)S(1)} collective-permute-done((bf16[768,384]{0,1:T(8,128)(2,1)S(1)}, bf16[768,384]{0,1:T(8,128)(2,1)S(1)}, u32[]{:S(2)}, u32[]{:S(2)}) %collective-permute-start.42) | collective-permute-done | bytes 589856 | tf_op jit(solution)/shard_map/ppermute | solution.py:97
  448.1 12.3 %collective-permute-done.29 = bf16[2,192,1152]{2,1,0:T(8,128)(2,1)S(1)} collective-permute-done((bf16[2,192,1152]{2,1,0:T(8,128)(2,1)S(1)}, bf16[2,192,1152]{2,1,0:T(8,128)(2,1)S(1)}, u32[]{:S(2)}, u32[]{:S(2)}) %collective-permute-start.29) | collective-permute-done | bytes 884768 | tf_op jit(solution)/shard_map/ppermute | solution.py:97
  464.6 6.3 %collective-permute-done.30 = bf16[192,1152]{1,0:T(8,128)(2,1)S(1)} collective-permute-done((bf16[192,1152]{1,0:T(8,128)(2,1)S(1)}, bf16[192,1152]{1,0:T(8,128)(2,1)S(1)}, u32[]{:S(2)}, u32[]{:S(2)}) %collective-permute-start.30) | collective-permute-done | bytes 442400 | tf_op jit(solution)/shard_map/ppermute | solution.py:97
  480.8 4.9 collective-permute-done.45
  509.8 6.0 %collective-permute-done.55 = f32[8,4096]{1,0:T(8,128)S(1)} collective-permute-done((f32[8,4096]{1,0:T(8,128)S(1)}, f32[8,4096]{1,0:T(8,128)S(1)}, u32[]{:S(2)}, u32[]{:S(2)}) %collective-permute-start.55) | collective-permute-done | bytes 131104 | tf_op jit(solution)/shard_map/ppermute | solution.py:97
  522.4 10.3 %add_add_fusion.3 = f32[640,768]{1,0:T(8,128)S(1)} fusion(f32[640,768]{1,0:T(8,128)} %copy-done.27, bf16[3072,768]{1,0:T(8,128)(2,1)} %place_weights.5, f32[768]{0:T(1024)S(1)} %copy-done.86, f32[640,3072]{1,0:T(8,128)} %copy-done.95, f32[3072]{0:T(1024)S(1)} %copy-done.83), kind=kOutput, calls=%fused_computation.50 | convolution fusion | flops 3040542720 | bytes 16530432 | tf_op jit(solution)/shard_map/dot_general | solution.py:361
  538.1 5.0 collective-permute-done.53
  (478 shorter events, 236.3 us)
Async XLA Ops:
  23.2 19.1 %collective-permute-start.2 = (bf16[2,2,192,384]{3,2,1,0:T(8,128)(2,1)S(1)}, bf16[2,2,192,384]{3,2,1,0:T(8,128)(2,1)}, u32[]{:S(2)}, u32[]{:S(2)}) collective-permute-start(bf16[2,2,192,384]{3,2,1,0:T(8,128)(2,1)S(1)} %pad_maximum_fusion.8), channel_id=1, source_target_pairs={{0,16},{8,24},{16,0},{24,8},{1,17},{9,25},{17,1},{25,9},{2,18},{10... | collective-permute-start | bytes 1769480 | tf_op jit(solution)/shard_map/ppermute | solution.py:97
  34.7 46.7 %collective-permute-start.22 = (bf16[192,384]{1,0:T(8,128)(2,1)}, bf16[192,384]{1,0:T(8,128)(2,1)}, u32[]{:S(2)}, u32[]{:S(2)}) collective-permute-start(bf16[192,384]{1,0:T(8,128)(2,1)} %pad_maximum_fusion.22), channel_id=1, source_target_pairs={{0,6},{1,7},{2,4},{3,5},{4,2},{5,3},{6,0},{7,1},{8,14},{9,15},{10,... | collective-permute-start | bytes 442376 | tf_op jit(solution)/shard_map/ppermute | solution.py:97
  37.4 44.9 %collective-permute-start.21 = (bf16[192,384]{1,0:T(8,128)(2,1)}, bf16[192,384]{1,0:T(8,128)(2,1)}, u32[]{:S(2)}, u32[]{:S(2)}) collective-permute-start(bf16[192,384]{1,0:T(8,128)(2,1)} %pad_maximum_fusion.22), channel_id=1, source_target_pairs={{0,4},{1,5},{2,6},{3,7},{4,0},{5,1},{6,2},{7,3},{8,12},{9,13},{10,... | collective-permute-start | bytes 442376 | tf_op jit(solution)/shard_map/ppermute | solution.py:97
  48.8 36.6 %collective-permute-start.9 = (bf16[192,384]{1,0:T(8,128)(2,1)}, bf16[192,384]{1,0:T(8,128)(2,1)}, u32[]{:S(2)}, u32[]{:S(2)}) collective-permute-start(bf16[192,384]{1,0:T(8,128)(2,1)} %convert_element_type.229), channel_id=1, source_target_pairs={{0,2},{1,3},{2,0},{3,1},{4,6},{5,7},{6,4},{7,5},{8,10},{9,11},{10,... | collective-permute-start | bytes 442376 | tf_op jit(solution)/shard_map/ppermute | solution.py:97
  50.7 37.9 %collective-permute-start.13 = (bf16[192,384]{1,0:T(8,128)(2,1)}, bf16[192,384]{1,0:T(8,128)(2,1)}, u32[]{:S(2)}, u32[]{:S(2)}) collective-permute-start(bf16[192,384]{1,0:T(8,128)(2,1)} %convert_element_type.229), channel_id=1, source_target_pairs={{0,6},{1,7},{2,4},{3,5},{4,2},{5,3},{6,0},{7,1},{8,14},{9,15},{10,... | collective-permute-start | bytes 442376 | tf_op jit(solution)/shard_map/ppermute | solution.py:97
  53.3 34.6 %collective-permute-start.19 = (bf16[2,192,384]{2,1,0:T(8,128)(2,1)}, bf16[2,192,384]{2,1,0:T(8,128)(2,1)S(1)}, u32[]{:S(2)}, u32[]{:S(2)}) collective-permute-start(bf16[2,192,384]{2,1,0:T(8,128)(2,1)} %get-tuple-element.145), channel_id=1, source_target_pairs={{0,8},{8,0},{16,24},{24,16},{1,9},{9,1},{17,25},{25,17},{2,10},{10... | collective-permute-start | bytes 884744 | tf_op jit(solution)/shard_map/ppermute | solution.py:97
  76.4 80.0 %all-to-all-start = ((bf16[4,640,576]{1,2,0:T(8,128)(2,1)}), bf16[4,640,576]{1,2,0:T(8,128)(2,1)}, u32[]{:S(2)}, u32[]{:S(2)}) async-start(bf16[4,640,576]{1,2,0:T(8,128)(2,1)} %bitcast.219), calls=%async_computation | async-start | bytes 5898240 | tf_op jit(solution)/shard_map/all_to_all | solution.py:135
  83.3 39.3 %collective-permute-start.23 = (bf16[2,192,384]{2,1,0:T(8,128)(2,1)S(1)}, bf16[2,192,384]{2,1,0:T(8,128)(2,1)S(1)}, u32[]{:S(2)}, u32[]{:S(2)}) collective-permute-start(bf16[2,192,384]{2,1,0:T(8,128)(2,1)S(1)} %get-tuple-element.143), channel_id=1, source_target_pairs={{0,16},{8,24},{16,0},{24,8},{1,17},{9,25},{17,1},{25,9},{2,18},{10... | collective-permute-start | bytes 884744 | tf_op jit(solution)/shard_map/ppermute | solution.py:97
  86.4 38.2 %collective-permute-start.10 = (bf16[2,192,384]{2,1,0:T(8,128)(2,1)S(1)}, bf16[2,192,384]{2,1,0:T(8,128)(2,1)S(1)}, u32[]{:S(2)}, u32[]{:S(2)}) collective-permute-start(bf16[2,192,384]{2,1,0:T(8,128)(2,1)S(1)} %get-tuple-element.141), channel_id=1, source_target_pairs={{0,8},{8,0},{16,24},{24,16},{1,9},{9,1},{17,25},{25,17},{2,10},{10... | collective-permute-start | bytes 884744 | tf_op jit(solution)/shard_map/ppermute | solution.py:97
  88.0 55.6 %collective-permute-start.20 = (bf16[2,2,192,384]{3,2,1,0:T(8,128)(2,1)S(1)}, bf16[2,2,192,384]{3,2,1,0:T(8,128)(2,1)S(1)}, u32[]{:S(2)}, u32[]{:S(2)}) collective-permute-start(bf16[2,2,192,384]{3,2,1,0:T(8,128)(2,1)S(1)} %pad_maximum_fusion.12), channel_id=1, source_target_pairs={{0,16},{8,24},{16,0},{24,8},{1,17},{9,25},{17,1},{25,9},{2,18},{10... | collective-permute-start | bytes 1769480 | tf_op jit(solution)/shard_map/ppermute | solution.py:97
  92.1 49.5 %collective-permute-start.14 = (bf16[2,192,384]{2,1,0:T(8,128)(2,1)S(1)}, bf16[2,192,384]{2,1,0:T(8,128)(2,1)S(1)}, u32[]{:S(2)}, u32[]{:S(2)}) collective-permute-start(bf16[2,192,384]{2,1,0:T(8,128)(2,1)S(1)} %get-tuple-element.139), channel_id=1, source_target_pairs={{0,16},{8,24},{16,0},{24,8},{1,17},{9,25},{17,1},{25,9},{2,18},{10... | collective-permute-start | bytes 884744 | tf_op jit(solution)/shard_map/ppermute | solution.py:97
  122.7 22.0 %collective-permute-start.24 = (bf16[2,2,192,384]{3,2,1,0:T(8,128)(2,1)S(1)}, bf16[2,2,192,384]{3,2,1,0:T(8,128)(2,1)S(1)}, u32[]{:S(2)}, u32[]{:S(2)}) collective-permute-start(bf16[2,2,192,384]{3,2,1,0:T(8,128)(2,1)S(1)} %pad_maximum_fusion.13), channel_id=1, source_target_pairs={{0,8},{8,0},{16,24},{24,16},{1,9},{9,1},{17,25},{25,17},{2,10},{10... | collective-permute-start | bytes 1769480 | tf_op jit(solution)/shard_map/ppermute | solution.py:97
  124.7 28.6 %collective-permute-start.11 = (bf16[2,2,192,384]{3,2,1,0:T(8,128)(2,1)S(1)}, bf16[2,2,192,384]{3,2,1,0:T(8,128)(2,1)S(1)}, u32[]{:S(2)}, u32[]{:S(2)}) collective-permute-start(bf16[2,2,192,384]{3,2,1,0:T(8,128)(2,1)S(1)} %pad_maximum_fusion.10), channel_id=1, source_target_pairs={{0,16},{8,24},{16,0},{24,8},{1,17},{9,25},{17,1},{25,9},{2,18},{10... | collective-permute-start | bytes 1769480 | tf_op jit(solution)/shard_map/ppermute | solution.py:97
  144.7 43.5 %collective-permute-start.25 = (bf16[4,2,192,384]{3,2,1,0:T(8,128)(2,1)}, bf16[4,2,192,384]{3,2,1,0:T(8,128)(2,1)}, u32[]{:S(2)}, u32[]{:S(2)}) collective-permute-start(bf16[4,2,192,384]{3,2,1,0:T(8,128)(2,1)} %pad_maximum_fusion.4.near_ref), channel_id=1, source_target_pairs={{0,1},{1,0},{2,3},{3,2},{4,5},{5,4},{6,7},{7,6},{8,9},{9,8},{10,11... | collective-permute-start | bytes 3538952 | tf_op jit(solution)/shard_map/ppermute | solution.py:97
  145.9 42.3 %collective-permute-start.26 = (bf16[4,2,192,384]{3,2,1,0:T(8,128)(2,1)}, bf16[4,2,192,384]{3,2,1,0:T(8,128)(2,1)}, u32[]{:S(2)}, u32[]{:S(2)}) collective-permute-start(bf16[4,2,192,384]{3,2,1,0:T(8,128)(2,1)} %pad_maximum_fusion.5.far_ref), channel_id=1, source_target_pairs={{0,1},{1,0},{2,3},{3,2},{4,5},{5,4},{6,7},{7,6},{8,9},{9,8},{10,11... | collective-permute-start | bytes 3538952 | tf_op jit(solution)/shard_map/ppermute | solution.py:97
  154.4 40.5 %collective-permute-start.16 = (bf16[4,2,192,384]{3,2,1,0:T(8,128)(2,1)}, bf16[4,2,192,384]{3,2,1,0:T(8,128)(2,1)}, u32[]{:S(2)}, u32[]{:S(2)}) collective-permute-start(bf16[4,2,192,384]{3,2,1,0:T(8,128)(2,1)} %pad_maximum_fusion.2.near_ref), channel_id=1, source_target_pairs={{0,1},{1,0},{2,3},{3,2},{4,5},{5,4},{6,7},{7,6},{8,9},{9,8},{10,11... | collective-permute-start | bytes 3538952 | tf_op jit(solution)/shard_map/ppermute | solution.py:97
  156.4 38.6 %collective-permute-start.17 = (bf16[4,2,192,384]{3,2,1,0:T(8,128)(2,1)}, bf16[4,2,192,384]{3,2,1,0:T(8,128)(2,1)}, u32[]{:S(2)}, u32[]{:S(2)}) collective-permute-start(bf16[4,2,192,384]{3,2,1,0:T(8,128)(2,1)} %pad_maximum_fusion.3.far_ref), channel_id=1, source_target_pairs={{0,1},{1,0},{2,3},{3,2},{4,5},{5,4},{6,7},{7,6},{8,9},{9,8},{10,11... | collective-permute-start | bytes 3538952 | tf_op jit(solution)/shard_map/ppermute | solution.py:97
  180.7 20.1 %all-to-all-start.1 = ((bf16[4,640,192]{1,2,0:T(8,128)(2,1)}), bf16[4,640,192]{1,2,0:T(8,128)(2,1)}, u32[]{:S(2)}, u32[]{:S(2)}) async-start(bf16[4,640,192]{1,2,0:T(8,128)(2,1)} %copy.67), calls=%async_computation.1 | async-start | bytes 1966080 | tf_op jit(solution)/shard_map/all_to_all | solution.py:135
  244.1 87.3 %all-to-all-start.2 = ((bf16[4,640,192]{1,2,0:T(8,128)(2,1)}), bf16[4,640,192]{1,2,0:T(8,128)(2,1)}, u32[]{:S(2)}, u32[]{:S(2)}) async-start(bf16[4,640,192]{1,2,0:T(8,128)(2,1)} %bitcast.229), calls=%async_computation.2 | async-start | bytes 1966080 | tf_op jit(solution)/shard_map/all_to_all | solution.py:135
  252.7 115.3 %collective-permute-start.37 = (bf16[2,192,1536]{2,1,0:T(8,128)(2,1)}, bf16[2,192,1536]{2,1,0:T(8,128)(2,1)}, u32[]{:S(2)}, u32[]{:S(2)}) collective-permute-start(bf16[2,192,1536]{2,1,0:T(8,128)(2,1)} %dynamic-slice_bitcast_fusion), channel_id=1, source_target_pairs={{0,16},{8,24},{16,0},{24,8},{1,17},{9,25},{17,1},{25,9},{2,18},{10... | collective-permute-start | bytes 3538952 | tf_op jit(solution)/shard_map/ppermute | solution.py:97
  255.9 121.9 %collective-permute-start.35 = (bf16[2,192,1536]{2,1,0:T(8,128)(2,1)}, bf16[2,192,1536]{2,1,0:T(8,128)(2,1)}, u32[]{:S(2)}, u32[]{:S(2)}) collective-permute-start(bf16[2,192,1536]{2,1,0:T(8,128)(2,1)} %dynamic-slice_bitcast_fusion.1), channel_id=1, source_target_pairs={{0,8},{8,0},{16,24},{24,16},{1,9},{9,1},{17,25},{25,17},{2,10},{10... | collective-permute-start | bytes 3538952 | tf_op jit(solution)/shard_map/ppermute | solution.py:97
  258.3 36.2 %collective-permute-start.33 = (bf16[2,192,384]{2,1,0:T(8,128)(2,1)}, bf16[2,192,384]{2,1,0:T(8,128)(2,1)}, u32[]{:S(2)}, u32[]{:S(2)}) collective-permute-start(bf16[2,192,384]{2,1,0:T(8,128)(2,1)} %dynamic-slice_bitcast_fusion.10), channel_id=1, source_target_pairs={{0,16},{8,24},{16,0},{24,8},{1,17},{9,25},{17,1},{25,9},{2,18},{10... | collective-permute-start | bytes 884744 | tf_op jit(solution)/shard_map/ppermute | solution.py:97
  259.7 37.4 %collective-permute-start.31 = (bf16[2,192,384]{2,1,0:T(8,128)(2,1)}, bf16[2,192,384]{2,1,0:T(8,128)(2,1)}, u32[]{:S(2)}, u32[]{:S(2)}) collective-permute-start(bf16[2,192,384]{2,1,0:T(8,128)(2,1)} %dynamic-slice_bitcast_fusion.11), channel_id=1, source_target_pairs={{0,8},{8,0},{16,24},{24,16},{1,9},{9,1},{17,25},{25,17},{2,10},{10... | collective-permute-start | bytes 884744 | tf_op jit(solution)/shard_map/ppermute | solution.py:97
  266.1 106.1 %collective-permute-start.41 = (bf16[2,768,384]{1,2,0:T(8,128)(2,1)}, bf16[2,768,384]{1,2,0:T(8,128)(2,1)}, u32[]{:S(2)}, u32[]{:S(2)}) collective-permute-start(bf16[2,768,384]{1,2,0:T(8,128)(2,1)} %bitcast.255), channel_id=1, source_target_pairs={{0,16},{8,24},{16,0},{24,8},{1,17},{9,25},{17,1},{25,9},{2,18},{10... | collective-permute-start | bytes 3538952 | tf_op jit(solution)/shard_map/ppermute | solution.py:97
  294.6 79.5 %collective-permute-start.39 = (bf16[2,768,384]{1,2,0:T(8,128)(2,1)}, bf16[2,768,384]{1,2,0:T(8,128)(2,1)}, u32[]{:S(2)}, u32[]{:S(2)}) collective-permute-start(bf16[2,768,384]{1,2,0:T(8,128)(2,1)} %bitcast.256), channel_id=1, source_target_pairs={{0,8},{8,0},{16,24},{24,16},{1,9},{9,1},{17,25},{25,17},{2,10},{10... | collective-permute-start | bytes 3538952 | tf_op jit(solution)/shard_map/ppermute | solution.py:97
  297.2 27.8 %collective-permute-start.34 = (bf16[192,384]{1,0:T(8,128)(2,1)S(1)}, bf16[192,384]{1,0:T(8,128)(2,1)S(1)}, u32[]{:S(2)}, u32[]{:S(2)}) collective-permute-start(bf16[192,384]{1,0:T(8,128)(2,1)S(1)} %dynamic-slice_bitcast_fusion.12), channel_id=1, source_target_pairs={{0,8},{8,0},{16,24},{24,16},{1,9},{9,1},{17,25},{25,17},{2,10},{10... | collective-permute-start | bytes 442376 | tf_op jit(solution)/shard_map/ppermute | solution.py:97
  362.0 69.9 %all-to-all-start.3 = ((bf16[4,640,576]{1,2,0:T(8,128)(2,1)}), bf16[4,640,576]{1,2,0:T(8,128)(2,1)}, u32[]{:S(2)}, u32[]{:S(2)}) async-start(bf16[4,640,576]{1,2,0:T(8,128)(2,1)} %copy.72), calls=%async_computation.3 | async-start | bytes 5898240 | tf_op jit(solution)/shard_map/all_to_all | solution.py:135
  370.1 57.7 %collective-permute-start.38 = (bf16[192,1536]{1,0:T(8,128)(2,1)S(1)}, bf16[192,1536]{1,0:T(8,128)(2,1)S(1)}, u32[]{:S(2)}, u32[]{:S(2)}) collective-permute-start(bf16[192,1536]{1,0:T(8,128)(2,1)S(1)} %dynamic-slice_bitcast_fusion.6), channel_id=1, source_target_pairs={{0,8},{8,0},{16,24},{24,16},{1,9},{9,1},{17,25},{25,17},{2,10},{10... | collective-permute-start | bytes 1769480 | tf_op jit(solution)/shard_map/ppermute | solution.py:97
  373.9 50.3 %collective-permute-start.42 = (bf16[768,384]{0,1:T(8,128)(2,1)S(1)}, bf16[768,384]{0,1:T(8,128)(2,1)S(1)}, u32[]{:S(2)}, u32[]{:S(2)}) collective-permute-start(bf16[768,384]{0,1:T(8,128)(2,1)S(1)} %dynamic-slice_bitcast_fusion.4), channel_id=1, source_target_pairs={{0,8},{8,0},{16,24},{24,16},{1,9},{9,1},{17,25},{25,17},{2,10},{10... | collective-permute-start | bytes 1769480 | tf_op jit(solution)/shard_map/ppermute | solution.py:97
  375.8 48.5 %collective-permute-start.40 = (bf16[768,384]{0,1:T(8,128)(2,1)S(1)}, bf16[768,384]{0,1:T(8,128)(2,1)S(1)}, u32[]{:S(2)}, u32[]{:S(2)}) collective-permute-start(bf16[768,384]{0,1:T(8,128)(2,1)S(1)} %dynamic-slice_bitcast_fusion.5), channel_id=1, source_target_pairs={{0,16},{8,24},{16,0},{24,8},{1,17},{9,25},{17,1},{25,9},{2,18},{10... | collective-permute-start | bytes 1769480 | tf_op jit(solution)/shard_map/ppermute | solution.py:97
  379.4 48.6 %collective-permute-start.36 = (bf16[192,1536]{1,0:T(8,128)(2,1)S(1)}, bf16[192,1536]{1,0:T(8,128)(2,1)S(1)}, u32[]{:S(2)}, u32[]{:S(2)}) collective-permute-start(bf16[192,1536]{1,0:T(8,128)(2,1)S(1)} %dynamic-slice_bitcast_fusion.7), channel_id=1, source_target_pairs={{0,16},{8,24},{16,0},{24,8},{1,17},{9,25},{17,1},{25,9},{2,18},{10... | collective-permute-start | bytes 1769480 | tf_op jit(solution)/shard_map/ppermute | solution.py:97
  443.6 20.6 %collective-permute-start.27 = (bf16[2,192,1152]{2,1,0:T(8,128)(2,1)S(1)}, bf16[2,192,1152]{2,1,0:T(8,128)(2,1)S(1)}, u32[]{:S(2)}, u32[]{:S(2)}) collective-permute-start(bf16[2,192,1152]{2,1,0:T(8,128)(2,1)S(1)} %dynamic-slice_bitcast_fusion.3), channel_id=1, source_target_pairs={{0,8},{8,0},{16,24},{24,16},{1,9},{9,1},{17,25},{25,17},{2,10},{10... | collective-permute-start | bytes 2654216 | tf_op jit(solution)/shard_map/ppermute | solution.py:97
  (134 other events, 1413.1 us)
